TPU v7x, 512 devices: a whole 4x4x16 slice. The times are simulated.
512 devices in a mesh: dom: 32 (over x, y, core), cls: 16 (over z).
Axes of the slice: x: 4, y: 4, z: 16, core: 2. Of those that a mesh axis runs over, the one named last changes fastest.
Arguments:
- particles: bfloat16 [4096, 128, 128], P(('dom', 'cls')), may hold values from -640 to 640
- centers: int32 [4096, 2], P(('dom', 'cls')), may hold values from -3 to 3
- rot_prior: int32 [4096], P(('dom', 'cls')), may hold values from 0 to 3
- groups: int32 [4096, 2], P(('dom', 'cls')), may hold values from 0 to 15, all different within a row; in each aligned block of 8 rows (0 to 7, 8 to 15, ...) at most 2 rows name the same one
- references: bfloat16 [320, 4, 16384], P('cls', None, 'dom'), may hold values from -1 to 1
Outputs:
- class_sums: float32 [16384, 320, 4], P('dom', 'cls')
- log_evidence: float32 [4096], P(('dom', 'cls'))
Inputs may be any that keep to these rules, and one draw needn't show every extreme that they name: `groups`: within the 8 rows of one device no class group is named by more than 2 particles, and the lists of one particle are distinct.
All inputs are finite; a program needn't handle non-finite values.
Results may differ from a plain program's by a relative error of at most 0.017.
Values may be sent and summed in bfloat16 or wider, within the bound.
A program may use at most 64 MiB of HBM per device.

v0:
```python
import jax
import jax.numpy as jnp
from jax import lax
from jax.sharding import PartitionSpec as P

LAMBDA = 1.0
NEG_BIG = -1e30


def per_device(particles, centers, rot_prior, groups, references):
    count, image_height, image_width = particles.shape
    topg = groups.shape[1]
    group_count = lax.axis_size("cls")
    slot_capacity = max(2, 2 * count * topg // group_count)
    slot_count = group_count * slot_capacity
    rotations = references.shape[1]
    reference_indices = references.shape[0] * rotations
    rows = jnp.arange(image_height, dtype=jnp.int32)
    cols = jnp.arange(image_width, dtype=jnp.int32)
    row_sel = (rows[None, None, :] == rows[None, :, None] + centers[:, 0, None, None]).astype(
        jnp.bfloat16
    )
    col_sel = (cols[None, None, :] == cols[None, :, None] + centers[:, 1, None, None]).astype(
        jnp.bfloat16
    )
    moved = jnp.einsum(
        "kua,kav->kuv", row_sel, particles, preferred_element_type=jnp.float32
    ).astype(jnp.bfloat16)
    centered = jnp.einsum(
        "kub,kvb->kuv", moved, col_sel, preferred_element_type=jnp.float32
    ).astype(jnp.bfloat16)
    flat_view = centered.reshape(count, image_height * image_width)
    hits = jnp.any(
        groups[:, :, None] == jnp.arange(group_count, dtype=jnp.int32)[None, None, :], axis=1
    ).astype(jnp.int32)
    places = jnp.cumsum(hits, axis=0) - 1
    owned = (hits.T[:, None, :] == 1) & (
        places.T[:, None, :] == jnp.arange(slot_capacity, dtype=jnp.int32)[None, :, None]
    )
    selection_mask = owned.astype(jnp.bfloat16)
    outgoing_image = jnp.einsum(
        "bno,oa->bna", selection_mask, flat_view, preferred_element_type=jnp.float32
    ).astype(jnp.bfloat16)
    meta_src = jnp.stack(
        [
            jnp.ones((count,), jnp.float32),
            rot_prior.astype(jnp.float32),
            jnp.arange(count, dtype=jnp.float32),
        ],
        axis=1,
    )
    send_meta = jnp.einsum("gck,km->gcm", owned.astype(jnp.float32), meta_src).astype(jnp.bfloat16)
    received_image, recv_meta = (
        lax.all_to_all(outgoing_image, "cls", split_axis=0, concat_axis=0, tiled=True),
        lax.all_to_all(send_meta, "cls", split_axis=0, concat_axis=0, tiled=True),
    )
    padded_image = jnp.pad(
        received_image.reshape(slot_count, image_height, image_width), ((0, 0), (1, 1), (1, 1))
    )
    particle_metadata = recv_meta.astype(jnp.float32)
    valid_mask = particle_metadata[:, :, 0].reshape(slot_count) > 0.5
    rotation_prior = particle_metadata[:, :, 1].reshape(slot_count)

    def window(leading_row, row_count, offset):
        shift_horizontal = offset // 3 - 1
        shift_vertical = offset % 3 - 1
        block_tile = lax.dynamic_slice(
            padded_image,
            (0, leading_row + 1 + shift_horizontal, 1 + shift_vertical),
            (slot_count, row_count, image_width),
        )
        return block_tile.reshape(slot_count, row_count * image_width)

    piece = lax.all_gather(references, "dom", axis=2, tiled=True)
    score_table = jnp.zeros((9, slot_count, reference_indices), jnp.float32)
    npix = piece.shape[2]
    panel = piece.reshape(reference_indices, npix)
    leading_row = jnp.int32(0) // image_width
    row_count = npix // image_width
    for offset in range(9):
        block_tile = window(leading_row, row_count, offset)
        score_table = score_table.at[offset].add(
            jnp.einsum("sp,jp->sj", block_tile, panel, preferred_element_type=jnp.float32)
        )
    norms = jnp.einsum("jp,jp->j", panel, panel, preferred_element_type=jnp.float32)
    score_table, norms = (score_table, norms)
    rot_of = (jnp.arange(reference_indices, dtype=jnp.int32) % rotations).astype(jnp.float32)
    delta = jnp.abs(rot_of[None, :] - rotation_prior[:, None])
    dist = jnp.minimum(delta, rotations - delta)
    loglik = score_table - 0.5 * norms[None, None, :] - LAMBDA * (dist**2)[None, :, :]
    slot_max = jnp.max(loglik, axis=(0, 2))
    slot_sum = jnp.sum(jnp.exp(loglik - slot_max[None, :, None]), axis=(0, 2))
    slot_max = jnp.where(valid_mask, slot_max, NEG_BIG)
    slot_sum = jnp.where(valid_mask, slot_sum, 0.0)
    back_max, back_sum = (
        lax.all_to_all(
            slot_max.reshape(group_count, slot_capacity),
            "cls",
            split_axis=0,
            concat_axis=0,
            tiled=True,
        ),
        lax.all_to_all(
            slot_sum.reshape(group_count, slot_capacity),
            "cls",
            split_axis=0,
            concat_axis=0,
            tiled=True,
        ),
    )
    part_max = jnp.max(jnp.where(owned, back_max[:, :, None], NEG_BIG), axis=(0, 1))
    part_sum = jnp.sum(
        jnp.where(
            owned,
            back_sum[:, :, None] * jnp.exp(back_max[:, :, None] - part_max[None, None, :]),
            0.0,
        ),
        axis=(0, 1),
    )
    log_evidence = part_max + jnp.log(part_sum)
    slot_ev = jnp.sum(jnp.where(owned, log_evidence[None, None, :], 0.0), axis=2)
    recv_ev = lax.all_to_all(slot_ev, "cls", split_axis=0, concat_axis=0, tiled=True).reshape(
        slot_count
    )
    posterior = jnp.where(
        valid_mask[None, :, None], jnp.exp(loglik - recv_ev[None, :, None]), 0.0
    ).astype(jnp.bfloat16)
    own_rows = image_height * image_width // lax.axis_size("dom")
    leading_row = jnp.int32(0) // image_width
    row_count = lax.axis_size("dom") * own_rows // image_width
    total = jnp.zeros((lax.axis_size("dom") * own_rows, reference_indices), jnp.float32)
    for offset in range(9):
        block_tile = window(leading_row, row_count, offset)
        total = total + jnp.einsum(
            "sp,sj->pj", block_tile, posterior[offset], preferred_element_type=jnp.float32
        )
    sums = lax.psum_scatter(
        total.astype(jnp.bfloat16), "dom", scatter_dimension=0, tiled=True
    ).astype(jnp.float32)
    return (sums.reshape(own_rows, references.shape[0], rotations), log_evidence)


def solution(mesh):
    placed = (
        P(("dom", "cls"), None, None),
        P(("dom", "cls"), None),
        P(("dom", "cls")),
        P(("dom", "cls"), None),
        P("cls", None, "dom"),
    )
    return jax.shard_map(
        per_device,
        mesh=mesh,
        in_specs=placed,
        out_specs=(P("dom", "cls", None), P(("dom", "cls"))),
        check_vma=False,
    )
```

profile of v0, /device:TPU:24, one launch (start us, length us, event | category | flops | bytes accessed | tf_op | source)
XLA Modules:
  0.0 283.0 jit_solution(8435589632452198391)
XLA Ops:
  10.3 15.2 %all-to-all-start.1 = ((bf16[16,2,3]{2,1,0:T(2,128)(2,1)}), bf16[16,2,3]{2,1,0:T(2,128)(2,1)S(1)}, u32[]{:S(2)}, u32[]{:S(2)}) async-start(bf16[16,2,3]{2,1,0:T(2,128)(2,1)} %copy.33), calls=%async_computation.1 | async-start | bytes 16384 | tf_op jit(solution)/shard_map/all_to_all | solution.py:55
  27.4 2.1 copy.32
  29.5 8.3 %all-to-all-done.1 = bf16[16,2,3]{2,1,0:T(2,128)(2,1)S(1)} async-done(((bf16[16,2,3]{2,1,0:T(2,128)(2,1)}), bf16[16,2,3]{2,1,0:T(2,128)(2,1)S(1)}, u32[]{:S(2)}, u32[]{:S(2)}) %all-to-all-start.1) | async-done | bytes 224 | tf_op jit(solution)/shard_map/all_to_all | solution.py:55
  37.8 3.8 %all-to-all-start = ((bf16[16,2,16384]{2,1,0:T(2,128)(2,1)}), bf16[16,2,16384]{2,1,0:T(2,128)(2,1)S(1)}, u32[]{:S(2)}, u32[]{:S(2)}) async-start(bf16[16,2,16384]{2,1,0:T(2,128)(2,1)} %copy.32), calls=%async_computation | async-start | bytes 2097152 | tf_op jit(solution)/shard_map/all_to_all | solution.py:54
  42.5 48.2 %all-to-all-done = bf16[16,2,16384]{2,1,0:T(2,128)(2,1)S(1)} async-done(((bf16[16,2,16384]{2,1,0:T(2,128)(2,1)}), bf16[16,2,16384]{2,1,0:T(2,128)(2,1)S(1)}, u32[]{:S(2)}, u32[]{:S(2)}) %all-to-all-start) | async-done | bytes 1048608 | tf_op jit(solution)/shard_map/all_to_all | solution.py:54
  90.7 1.2 reshape.502
  92.8 4.4 %pad_slice_fusion = (bf16[32,128,128]{2,1,0:T(8,128)(2,1)}, bf16[32,128,128]{2,1,0:T(8,128)(2,1)}, bf16[32,128,128]{2,1,0:T(8,128)(2,1)}, bf16[32,128,128]{2,1,0...) fusion(bf16[32,128,128]{2,1,0:T(8,128)(2,1)S(1)} %reshape.493), kind=kLoop, calls=%fused_computation.12 | loop fusion | bytes 9437184 | tf_op jit(solution)/shard_map/dynamic_slice | solution.py:67
  97.2 3.5 %reshape.495 = bf16[80,16384]{1,0:T(8,128)(2,1)S(1)} reshape(bf16[20,4,16384]{2,1,0:T(4,128)(2,1)} %all-gather.2.cloned.1.call-done) | data formatting | bytes 5242880 | tf_op jit(solution)/shard_map/reshape | solution.py:77
  113.5 8.1 %all-to-all-start.2 = ((f32[16,1,2]{2,1,0:T(1,128)}), f32[16,1,2]{2,1,0:T(1,128)S(1)}, u32[]{:S(2)}, u32[]{:S(2)}) async-start(f32[16,1,2]{2,1,0:T(1,128)} %copy.36), calls=%async_computation.2 | async-start | bytes 16384 | tf_op jit(solution)/shard_map/all_to_all | solution.py:96
  122.3 11.7 %all-to-all-done.2 = f32[16,1,2]{2,1,0:T(1,128)S(1)} async-done(((f32[16,1,2]{2,1,0:T(1,128)}), f32[16,1,2]{2,1,0:T(1,128)S(1)}, u32[]{:S(2)}, u32[]{:S(2)}) %all-to-all-start.2) | async-done | bytes 160 | tf_op jit(solution)/shard_map/all_to_all | solution.py:96
  134.0 3.6 %all-to-all-start.3 = ((f32[16,1,2]{2,1,0:T(1,128)}), f32[16,1,2]{2,1,0:T(1,128)S(1)}, u32[]{:S(2)}, u32[]{:S(2)}) async-start(f32[16,1,2]{2,1,0:T(1,128)} %copy.39), calls=%async_computation.3 | async-start | bytes 16384 | tf_op jit(solution)/shard_map/all_to_all | solution.py:103
  137.8 12.0 %all-to-all-done.3 = f32[16,1,2]{2,1,0:T(1,128)S(1)} async-done(((f32[16,1,2]{2,1,0:T(1,128)}), f32[16,1,2]{2,1,0:T(1,128)S(1)}, u32[]{:S(2)}, u32[]{:S(2)}) %all-to-all-start.3) | async-done | bytes 160 | tf_op jit(solution)/shard_map/all_to_all | solution.py:103
  150.8 3.5 %all-to-all-start.4 = ((f32[16,1,2]{2,1,0:T(1,128)}), f32[16,1,2]{2,1,0:T(1,128)S(1)}, u32[]{:S(2)}, u32[]{:S(2)}) async-start(f32[16,1,2]{2,1,0:T(1,128)} %copy.41), calls=%async_computation.4 | async-start | bytes 16384 | tf_op jit(solution)/shard_map/all_to_all | solution.py:122
  154.5 12.1 %all-to-all-done.4 = f32[16,1,2]{2,1,0:T(1,128)S(1)} async-done(((f32[16,1,2]{2,1,0:T(1,128)}), f32[16,1,2]{2,1,0:T(1,128)S(1)}, u32[]{:S(2)}, u32[]{:S(2)}) %all-to-all-start.4) | async-done | bytes 160 | tf_op jit(solution)/shard_map/all_to_all | solution.py:122
  168.0 2.2 fusion.31
  170.2 1.2 convolution_add_fusion.7
  171.5 1.2 convolution_add_fusion.6
  172.7 1.2 convolution_add_fusion.5
  175.1 1.2 convolution_add_fusion.3
  176.4 1.2 convolution_add_fusion.2
  177.6 1.2 convolution_add_fusion.1
  178.8 2.5 fusion
  181.3 93.3 %reduce-scatter.2.cloned.1.call-done = bf16[512,80]{0,1:T(8,128)(2,1)} async-done(((bf16[16384,80]{0,1:T(8,128)(2,1)}), bf16[512,80]{0,1:T(8,128)(2,1)}) %reduce-scatter.2.cloned.1.call-update) | async-done | bytes 81936 | tf_op jit(solution)/shard_map/reduce_scatter | solution.py:137
  274.6 1.6 reshape.515
  (99 shorter events, 24.3 us)
Async XLA Ops:
  7.2 19.2 %copy-start = (bf16[8,128,128]{2,1,0:T(8,128)(2,1)S(1)}, bf16[8,128,128]{2,1,0:T(8,128)(2,1)}, u32[]{:S(2)}) copy-start(bf16[8,128,128]{2,1,0:T(8,128)(2,1)} %param.23) | copy-start | bytes 786436
  7.2 90.0 %all-gather.2.cloned.1.call-start = ((), (), s32[]{:S(2)}) async-start(), calls=%async_computation.6 | async-start | bytes 2703360 | tf_op jit(solution)/shard_map/all_gather | solution.py:74
  10.3 27.6 %all-to-all-start.1 = ((bf16[16,2,3]{2,1,0:T(2,128)(2,1)}), bf16[16,2,3]{2,1,0:T(2,128)(2,1)S(1)}, u32[]{:S(2)}, u32[]{:S(2)}) async-start(bf16[16,2,3]{2,1,0:T(2,128)(2,1)} %copy.33), calls=%async_computation.1 | async-start | bytes 16384 | tf_op jit(solution)/shard_map/all_to_all | solution.py:55
  37.8 52.9 %all-to-all-start = ((bf16[16,2,16384]{2,1,0:T(2,128)(2,1)}), bf16[16,2,16384]{2,1,0:T(2,128)(2,1)S(1)}, u32[]{:S(2)}, u32[]{:S(2)}) async-start(bf16[16,2,16384]{2,1,0:T(2,128)(2,1)} %copy.32), calls=%async_computation | async-start | bytes 2097152 | tf_op jit(solution)/shard_map/all_to_all | solution.py:54
  100.7 1.2 copy-start.1
  100.7 2.4 copy-start.14
  103.1 1.2 copy-start.12
  104.2 1.3 copy-start.10
  105.3 1.3 copy-start.16
  106.6 1.2 copy-start.8
  107.4 1.4 copy-start.6
  108.8 1.2 copy-start.4
  109.8 1.3 copy-start.2
  113.5 20.5 %all-to-all-start.2 = ((f32[16,1,2]{2,1,0:T(1,128)}), f32[16,1,2]{2,1,0:T(1,128)S(1)}, u32[]{:S(2)}, u32[]{:S(2)}) async-start(f32[16,1,2]{2,1,0:T(1,128)} %copy.36), calls=%async_computation.2 | async-start | bytes 16384 | tf_op jit(solution)/shard_map/all_to_all | solution.py:96
  134.0 15.8 %all-to-all-start.3 = ((f32[16,1,2]{2,1,0:T(1,128)}), f32[16,1,2]{2,1,0:T(1,128)S(1)}, u32[]{:S(2)}, u32[]{:S(2)}) async-start(f32[16,1,2]{2,1,0:T(1,128)} %copy.39), calls=%async_computation.3 | async-start | bytes 16384 | tf_op jit(solution)/shard_map/all_to_all | solution.py:103
  150.0 20.2 %copy-start.18 = (f32[8]{0:T(128)}, f32[8]{0:T(128)S(1)}, u32[]{:S(2)}) copy-start(f32[8]{0:T(128)S(1)} %log_add_fusion) | copy-start | bytes 100
  150.8 15.8 %all-to-all-start.4 = ((f32[16,1,2]{2,1,0:T(1,128)}), f32[16,1,2]{2,1,0:T(1,128)S(1)}, u32[]{:S(2)}, u32[]{:S(2)}) async-start(f32[16,1,2]{2,1,0:T(1,128)} %copy.41), calls=%async_computation.4 | async-start | bytes 16384 | tf_op jit(solution)/shard_map/all_to_all | solution.py:122
  154.3 120.3 %reduce-scatter.2.cloned.1.call-start = ((), (), s32[]{:S(2)}) async-start(), calls=%async_computation.7 | async-start | bytes 2703360 | tf_op jit(solution)/shard_map/reduce_scatter | solution.py:137
  168.0 2.2 copy-start.15
  170.2 1.2 copy-start.13
  171.4 1.2 copy-start.11
  172.7 1.2 copy-start.17
  173.9 1.2 copy-start.9
  175.1 1.2 copy-start.7
  (2 other events, 2.4 us)
Sparse Core Ops, SparseCore 0:
  11.1 64.9 all-gather.1
  181.4 93.1 reduce-scatter.1
where the time goes:
time: 284 us; the launch traced here: 283 us
  waiting for transfers between devices  186 us (65%)
  starting transfers between devices  34.4 us (12%)
  matrix products  22.7 us (8%)
  local copies, waits for them, and re-layouts  21.2 us (7%)
  between operations  14.4 us (5%)
  other arithmetic  4.1 us (1%)
    reduce_scatter x1, waiting for transfers between devices, per_device(): lax.psum_scatter(total.astype(jnp.bfloat16), 'dom', scatter_dimension=0,...  93.3 us
    all_to_all x1, waiting for transfers between devices, per_device(): lax.all_to_all(outgoing_image, 'cls', split_axis=0, concat_axis=0, tiled=...  48.2 us
    all_to_all x1, starting transfers between devices, per_device(): lax.all_to_all(send_meta, 'cls', split_axis=0, concat_axis=0, tiled=True)  15.2 us
    dot_general x9, matrix products, per_device(): jnp.einsum('sp,sj->pj', block_tile, posterior[offset], preferred_element_...  12.5 us
    all_to_all x1, waiting for transfers between devices, per_device(): lax.all_to_all(slot_ev, 'cls', split_axis=0, concat_axis=0, tiled=True)  12.1 us
    all_to_all x1, waiting for transfers between devices, per_device(): lax.all_to_all(slot_sum.reshape(group_count, slot_capacity), 'cls', split...  12 us
    all_to_all x1, waiting for transfers between devices, per_device(): lax.all_to_all(slot_max.reshape(group_count, slot_capacity), 'cls', split...  11.7 us
    dot_general x9, matrix products, per_device(): jnp.einsum('sp,jp->sj', block_tile, panel, preferred_element_type=jnp.flo...  8.96 us
  transfers between devices with their start and end apart: 7, of which 6 were waited for; matrix products, arithmetic and copies ran while one was open for 5% of the time, Pallas kernels for 0%

commit v1 on v0

v1 whole, which is shorter than its diff:
```python
import functools

import jax
import jax.numpy as jnp
from jax import lax
from jax.experimental import pallas as pl
from jax.experimental.pallas import tpu as pltpu
from jax.sharding import PartitionSpec as P

LAMBDA = 1.0
NEG_BIG = -1e30
LANES = 128
VMEM = pl.BlockSpec(memory_space=pltpu.VMEM)
MESH = pl.DeviceIdType.MESH


def remote(src, dst, send_sem, recv_sem, peer):
    return pltpu.make_async_remote_copy(
        src_ref=src, dst_ref=dst, send_sem=send_sem, recv_sem=recv_sem, device_id=peer, device_id_type=MESH
    )


def greet(dom, ring):
    barrier = pltpu.get_barrier_semaphore()
    total = 0
    if dom:
        me = lax.axis_index("dom")

        def one(k, carry):
            pl.semaphore_signal(barrier, inc=1, device_id={"dom": lax.rem(me + k, dom)}, device_id_type=MESH)
            return carry

        lax.fori_loop(1, dom, one, 0)
        total += dom - 1
    if ring:
        z = lax.axis_index("cls")
        for step in (1, ring - 1):
            pl.semaphore_signal(barrier, inc=1, device_id={"cls": lax.rem(z + step, ring)}, device_id_type=MESH)
        total += 2
    pl.semaphore_wait(barrier, total)


def chunks(blocks):
    half = (blocks + 1) // 2
    return [(0, half), (half, blocks - half)]


def spread_kernel(dom, ring, refs, imgs, all_refs, all_imgs, rs, rr, ls, lr, ds, dr, local):
    d = lax.axis_index("dom")
    z = lax.axis_index("cls")
    right, left = lax.rem(z + 1, ring), lax.rem(z + ring - 1, ring)
    greet(dom, ring)
    parts = chunks(refs.shape[0])
    steps_r = ring // 2
    steps_l = ring - 1 - steps_r
    own = pltpu.make_async_copy(refs, all_refs.at[z], local.at[0])
    own.start()
    mine = pltpu.make_async_copy(imgs.at[d], all_imgs.at[d], local.at[1])
    mine.start()

    def hop(step, c, to_right):
        first, size = parts[c]
        piece = lax.rem(z + ring - step, ring) if to_right else lax.rem(z + step, ring)
        block = all_refs.at[piece, pl.ds(first, size)]
        src = refs.at[pl.ds(first, size)] if step == 0 else block
        send, recv = (rs, rr) if to_right else (ls, lr)
        return remote(src, block, send.at[step, c], recv.at[step, c], {"cls": right if to_right else left})

    sent = {}
    for c in range(2):
        for to_right in (True, False):
            sent[0, c, to_right] = hop(0, c, to_right)
            sent[0, c, to_right].start()

    def strip(k):
        peer = lax.rem(d + k, dom)
        return remote(imgs.at[peer], all_imgs.at[d], ds.at[k], dr.at[k], {"dom": peer})

    def start(k, carry):
        strip(k).start()
        return carry

    def finish(k, carry):
        strip(k).wait()
        return carry

    lax.fori_loop(1, dom, start, 0)
    for step in range(1, steps_r):
        for c in range(2):
            for to_right in (True, False):
                if step < (steps_r if to_right else steps_l):
                    sent[step - 1, c, to_right].wait_recv()
                    sent[step, c, to_right] = hop(step, c, to_right)
                    sent[step, c, to_right].start()
    for c in range(2):
        sent[steps_r - 1, c, True].wait_recv()
        sent[steps_l - 1, c, False].wait_recv()
    lax.fori_loop(1, dom, finish, 0)
    for copy in sent.values():
        copy.wait_send()
    own.wait()
    mine.wait()


def spread(dom, ring, refs, imgs):
    half = ring // 2
    sem = pltpu.SemaphoreType.DMA
    return pl.pallas_call(
        functools.partial(spread_kernel, dom, ring),
        out_shape=(
            jax.ShapeDtypeStruct((ring,) + refs.shape, refs.dtype),
            jax.ShapeDtypeStruct(imgs.shape, imgs.dtype),
        ),
        in_specs=[VMEM] * 2,
        out_specs=(VMEM, VMEM),
        scratch_shapes=[sem((half, 2))] * 4 + [sem((dom,)), sem((dom,)), sem((2,))],
        compiler_params=pltpu.CompilerParams(collective_id=0, has_side_effects=True),
    )(refs, imgs)


def score_kernel(groups, dim_j, refs, imgs, meta, shifted, out, score, bias):
    dom, strip, count, width = imgs.shape
    own_rows = strip - 3
    slots = dom * count
    lane = lax.broadcasted_iota(jnp.int32, (slots, width), 1)
    for h in range(own_rows + 2):
        mid = imgs[:, h].astype(jnp.float32).reshape(slots, width)
        before = jnp.where(lane == 0, 0.0, pltpu.roll(mid, 1, axis=1))
        after = jnp.where(lane == width - 1, 0.0, pltpu.roll(mid, width - 1, axis=1))
        for sy, plane in enumerate((before, mid, after)):
            plane = plane.astype(jnp.bfloat16)
            for sx in range(3):
                r = h - sx
                if 0 <= r < own_rows:
                    shifted[3 * sx + sy, :, r * width:(r + 1) * width] = plane
    names = [jnp.broadcast_to(meta[t:t + 1, :], (dim_j, slots)) for t in range(2)]

    def add_norm(g, carry):
        rows = pl.ds(pl.multiple_of(g * dim_j, 16), dim_j)
        block = refs[rows, :].astype(jnp.float32)
        norm = jnp.sum(block * block, axis=1, keepdims=True)
        for t in range(2):
            bias[t] = jnp.where(names[t] == g, -0.5 * norm, bias[t])
        return carry

    bias[...] = jnp.zeros_like(bias)
    lax.fori_loop(0, groups, add_norm, 0)

    def one(w, carry):
        score[...] = lax.dot_general(
            refs[...], shifted[w], (((1,), (1,)), ((), ())), preferred_element_type=jnp.float32
        )
        for t in range(2):
            picked = jnp.zeros((dim_j, slots), jnp.float32)
            for g in range(groups):
                picked = jnp.where(names[t] == g, score[g * dim_j:(g + 1) * dim_j, :], picked)
            start = pl.multiple_of((t * 9 + w) * dim_j, 16)
            out[pl.ds(start, dim_j), :] = picked + bias[t]
        return carry

    lax.fori_loop(0, 9, one, 0)
    used = 18 * dim_j
    if out.shape[0] > used:
        out[used:, :] = jnp.zeros((out.shape[0] - used, slots), jnp.float32)


def evidence_kernel(dom, rotations, used, part, meta, like, stat, landed, s0, r0, s1, r1, s2, r2):
    d = lax.axis_index("dom")
    greet(dom, 0)

    def to(k):
        return lax.rem(d + k, dom)

    def scatter(k):
        return remote(part.at[to(k)], landed.at[d], s0.at[k], r0.at[k], {"dom": to(k)})

    def spread_like(k):
        return remote(like.at[d], like.at[d], s1.at[k], r1.at[k], {"dom": to(k)})

    def spread_stat(k):
        return remote(stat.at[d], stat.at[d], s2.at[k], r2.at[k], {"dom": to(k)})

    def start(k, carry):
        scatter(k).start()
        return carry

    lax.fori_loop(1, dom, start, 0)

    def take(k, carry):
        scatter(k).wait_recv()
        return carry + landed[lax.rem(d + dom - k, dom)]

    total = lax.fori_loop(1, dom, take, part[d])
    row = lax.broadcasted_iota(jnp.int32, total.shape, 0)
    prior = jnp.broadcast_to(meta[2:3, :], total.shape)
    delta = jnp.abs(row % rotations - prior)
    dist = jnp.minimum(delta, rotations - delta).astype(jnp.float32)
    valid = row + d * total.shape[0] < used
    loglik = jnp.where(valid, total - LAMBDA * dist * dist, NEG_BIG)
    top = jnp.max(loglik, axis=0, keepdims=True)
    value = jnp.where(valid, jnp.exp(loglik - top), 0.0)
    like[d] = value.astype(jnp.bfloat16)
    mass = jnp.sum(value, axis=0, keepdims=True)
    pick = lax.broadcasted_iota(jnp.int32, stat.shape[1:], 0)
    stat[d] = jnp.where(pick == 0, top, mass)

    def give(k, carry):
        scatter(k).wait_send()
        spread_like(k).start()
        spread_stat(k).start()
        return carry

    lax.fori_loop(1, dom, give, 0)

    def finish(k, carry):
        spread_like(k).wait()
        spread_stat(k).wait()
        return carry

    lax.fori_loop(1, dom, finish, 0)


def sums_kernel(groups, dim_j, like, stat, meta, shifted, out, evidence, post, dense, acc):
    dom, rows, slots = like.shape
    top = stat[:, 0, :]
    mass = stat[:, 1, :]
    peak = jnp.max(top, axis=0, keepdims=True)
    total = jnp.sum(mass * jnp.exp(top - peak), axis=0, keepdims=True)
    ev = peak + jnp.log(total)
    evidence[...] = jnp.broadcast_to(ev, evidence.shape)

    def scale(k, carry):
        factor = jnp.exp(stat[k, 0:1, :] - ev)
        post[pl.ds(pl.multiple_of(k * rows, 16), rows), :] = (like[k].astype(jnp.float32) * factor).astype(jnp.bfloat16)
        return carry

    lax.fori_loop(0, dom, scale, 0)
    names = [jnp.broadcast_to(meta[t:t + 1, :], (dim_j, slots)) for t in range(2)]

    def one(w, carry):
        p0 = post[pl.ds(pl.multiple_of(w * dim_j, 16), dim_j), :].astype(jnp.float32)
        p1 = post[pl.ds(pl.multiple_of((9 + w) * dim_j, 16), dim_j), :].astype(jnp.float32)
        for g in range(groups):
            weight = jnp.where(names[0] == g, p0, jnp.where(names[1] == g, p1, 0.0))
            dense[g * dim_j:(g + 1) * dim_j, :] = weight.astype(jnp.bfloat16)
        acc[...] += jnp.dot(dense[...], shifted[w], preferred_element_type=jnp.float32)
        return carry

    acc[...] = jnp.zeros_like(acc)
    lax.fori_loop(0, 9, one, 0)
    out[...] = acc[...].astype(jnp.bfloat16)


def collect_kernel(ring, part, out, from_left, from_right, rs, rr, ls, lr):
    z = lax.axis_index("cls")
    right, left = lax.rem(z + 1, ring), lax.rem(z + ring - 1, ring)
    greet(0, ring)
    parts = chunks(part.shape[1])
    steps_r = ring // 2
    steps_l = ring - 1 - steps_r
    sent = {}
    for step in range(steps_r):
        for c, (first, size) in enumerate(parts):
            cut = pl.ds(first, size)
            for to_right in (True, False):
                if step >= (steps_r if to_right else steps_l):
                    continue
                hold = from_left if to_right else from_right
                owner = lax.rem(z + steps_r - step, ring) if to_right else lax.rem(z + ring - steps_l + step, ring)
                src = part.at[owner, cut]
                if step:
                    sent[step - 1, c, to_right].wait_recv()
                    hold[step - 1, cut] = (
                        hold[step - 1, cut].astype(jnp.float32) + part[owner, cut].astype(jnp.float32)
                    ).astype(jnp.bfloat16)
                    src = hold.at[step - 1, cut]
                send, recv = (rs, rr) if to_right else (ls, lr)
                copy = remote(
                    src, hold.at[step, cut], send.at[step, c], recv.at[step, c],
                    {"cls": right if to_right else left},
                )
                copy.start()
                sent[step, c, to_right] = copy
    for c, (first, size) in enumerate(parts):
        cut = pl.ds(first, size)
        sent[steps_r - 1, c, True].wait_recv()
        sent[steps_l - 1, c, False].wait_recv()
        out[cut] = (
            part[z, cut].astype(jnp.float32)
            + from_left[steps_r - 1, cut].astype(jnp.float32)
            + from_right[steps_l - 1, cut].astype(jnp.float32)
        )
    for copy in sent.values():
        copy.wait_send()


def per_device(particles, centers, rot_prior, groups, references):
    count, height, width = particles.shape
    dom = lax.axis_size("dom")
    ring = lax.axis_size("cls")
    rotations = references.shape[1]
    dim_j = references.shape[0] * rotations
    own_rows = height // dom
    pixels = own_rows * width
    strip = own_rows + 2
    slots = dom * count
    sem = pltpu.SemaphoreType.DMA

    line = jnp.arange(dom * strip, dtype=jnp.int32)
    line = (line // strip) * own_rows + line % strip - 1
    inside = (line >= 0) & (line < height)
    rows = jnp.arange(height, dtype=jnp.int32)
    cols = jnp.arange(width, dtype=jnp.int32)
    row_sel = (
        (rows[None, None, :] == line[None, :, None] + centers[:, 0, None, None]) & inside[None, :, None]
    ).astype(jnp.bfloat16)
    col_sel = (cols[None, None, :] == cols[None, :, None] + centers[:, 1, None, None]).astype(jnp.bfloat16)
    moved = jnp.einsum("kua,kav->kuv", row_sel, particles, preferred_element_type=jnp.float32).astype(jnp.bfloat16)
    strips = jnp.einsum("kub,kvb->kuv", moved, col_sel, preferred_element_type=jnp.float32).astype(jnp.bfloat16)
    strips = strips.reshape(count, dom, strip, width).transpose(1, 2, 0, 3)
    notes = jnp.concatenate([groups, rot_prior[:, None]], axis=1).astype(jnp.bfloat16)
    notes = jnp.pad(notes, ((0, 0), (0, width - notes.shape[1])))
    strips = jnp.concatenate([strips, jnp.broadcast_to(notes, (dom, 1, count, width))], axis=1)

    refs = references.reshape(dim_j // 16, 16, pixels)
    all_refs, all_strips = spread(dom, ring, refs, strips)
    meta = all_strips[:, strip].reshape(slots, width)[:, :8].T.astype(jnp.int32)

    share = -(-18 * dim_j // (16 * dom)) * 16
    shifted, part = pl.pallas_call(
        functools.partial(score_kernel, ring, dim_j),
        out_shape=(
            jax.ShapeDtypeStruct((9, slots, pixels), jnp.bfloat16),
            jax.ShapeDtypeStruct((dom * share, slots), jnp.float32),
        ),
        in_specs=[VMEM] * 3,
        out_specs=(VMEM, VMEM),
        scratch_shapes=[
            pltpu.VMEM((ring * dim_j, slots), jnp.float32),
            pltpu.VMEM((2, dim_j, slots), jnp.float32),
        ],
    )(all_refs.reshape(ring * dim_j, pixels), all_strips, meta)

    like, stat = pl.pallas_call(
        functools.partial(evidence_kernel, dom, rotations, 18 * dim_j),
        out_shape=(
            jax.ShapeDtypeStruct((dom, share, slots), jnp.bfloat16),
            jax.ShapeDtypeStruct((dom, 8, slots), jnp.float32),
        ),
        in_specs=[VMEM] * 2,
        out_specs=(VMEM, VMEM),
        scratch_shapes=[pltpu.VMEM((dom, share, slots), jnp.float32)] + [sem((dom,))] * 6,
        compiler_params=pltpu.CompilerParams(collective_id=1, has_side_effects=True),
    )(part.reshape(dom, share, slots), meta)

    sums, evidence = pl.pallas_call(
        functools.partial(sums_kernel, ring, dim_j),
        out_shape=(
            jax.ShapeDtypeStruct((ring * dim_j, pixels), jnp.bfloat16),
            jax.ShapeDtypeStruct((8, slots), jnp.float32),
        ),
        in_specs=[VMEM] * 4,
        out_specs=(VMEM, VMEM),
        scratch_shapes=[
            pltpu.VMEM((dom * share, slots), jnp.bfloat16),
            pltpu.VMEM((ring * dim_j, slots), jnp.bfloat16),
            pltpu.VMEM((ring * dim_j, pixels), jnp.float32),
        ],
    )(like, stat, meta, shifted)

    half = ring // 2
    block = (dim_j // 16, 16, pixels)
    total = pl.pallas_call(
        functools.partial(collect_kernel, ring),
        out_shape=jax.ShapeDtypeStruct(block, jnp.float32),
        in_specs=[VMEM],
        out_specs=VMEM,
        scratch_shapes=[pltpu.VMEM((half,) + block, jnp.bfloat16)] * 2 + [sem((half, 2))] * 4,
        compiler_params=pltpu.CompilerParams(collective_id=2, has_side_effects=True),
    )(sums.reshape((ring,) + block))
    class_sums = total.reshape(references.shape[0], rotations, pixels).transpose(2, 0, 1)
    log_evidence = lax.dynamic_slice(evidence[0], (lax.axis_index("dom") * count,), (count,))
    return class_sums, log_evidence


def solution(mesh):
    placed = (
        P(("dom", "cls"), None, None),
        P(("dom", "cls"), None),
        P(("dom", "cls")),
        P(("dom", "cls"), None),
        P("cls", None, "dom"),
    )
    return jax.shard_map(
        per_device,
        mesh=mesh,
        in_specs=placed,
        out_specs=(P("dom", "cls", None), P(("dom", "cls"))),
        check_vma=False,
    )
```

time: 284 us -> 160 us (0.56)
  waiting for transfers between devices: 186 us -> 0 us
  Pallas kernels: 0 us -> 151 us
  starting transfers between devices: 34.4 us -> 0 us
  matrix products: 22.7 us -> 0.61 us
  local copies, waits for them, and re-layouts: 21.2 us -> 5.63 us
  between operations: 14.4 us -> 0.74 us
    pallas_call x0 -> x5, Pallas kernels: none -> 151 us  [the longest x1 56.6 us: per_device(): pl.pallas_call(functools.partial(evidence_kernel, dom, rotations, 18 * di...]
    reduce_scatter x1 -> x0, waiting for transfers between devices: 93.3 us -> none  [per_device(): lax.psum_scatter(total.astype(jnp.bfloat16), 'dom', scatter_dimension=0,...]
    all_to_all x5 -> x0, waiting for transfers between devices: 92.3 us -> none  [the longest x1 48.2 us: per_device(): lax.all_to_all(outgoing_image, 'cls', split_axis=0, concat_axis=0, tiled=...]
    all_to_all x5 -> x0, starting transfers between devices: 34.3 us -> none  [the longest x1 15.2 us: per_device(): lax.all_to_all(send_meta, 'cls', split_axis=0, concat_axis=0, tiled=True)]
    dot_general x20 -> x0, matrix products: 22.1 us -> none  [the longest x9 12.5 us: per_device(): jnp.einsum('sp,sj->pj', block_tile, posterior[offset], preferred_element_...]
    reshape x5 -> x2, local copies, waits for them, and re-layouts: 7.27 us -> 2.29 us  [the longest x1 1.63 us: per_device(): total.reshape(references.shape[0], rotations, pixels).transpose(2, 0, 1)]
    dynamic_slice x1, local copies, waits for them, and re-layouts: 4.43 us -> 0.58 us  [per_device(): lax.dynamic_slice(evidence[0], (lax.axis_index('dom') * count,), (count,))]
  transfers between devices with their start and end apart: 7 -> 0, of which waited for: 6 -> 0; matrix products, arithmetic and copies ran while one was open for 5% -> 0% of each run, Pallas kernels for 0% -> 0%
where the time goes in v1:
time: 160 us; the launch traced here: 159 us
  Pallas kernels  151 us (94%)
  local copies, waits for them, and re-layouts  5.63 us (4%)
  other arithmetic  1.64 us (1%)
    pallas_call x1, Pallas kernels, per_device(): pl.pallas_call(functools.partial(evidence_kernel, dom, rotations, 18 * di...  56.6 us
    pallas_call x1, Pallas kernels, spread(): pl.pallas_call(functools.partial(spread_kernel, dom, ring), out_shape=(ja...  44.8 us
    pallas_call x1, Pallas kernels, per_device(): pl.pallas_call(functools.partial(collect_kernel, ring), out_shape=jax.Sha...  31.3 us
    pallas_call x1, Pallas kernels, per_device(): pl.pallas_call(functools.partial(score_kernel, ring, dim_j), out_shape=(j...  9.58 us
    pallas_call x1, Pallas kernels, per_device(): pl.pallas_call(functools.partial(sums_kernel, ring, dim_j), out_shape=(ja...  8.45 us

profile of v1, /device:TPU:24, one launch (start us, length us, event | category | flops | bytes accessed | tf_op | source)
XLA Modules:
  0.0 159.4 jit_solution(5289379389316515464)
XLA Ops:
  0.6 0.0 copy-start
  0.6 0.0 copy-start.2
  0.7 0.0 copy-start.3
  0.7 0.8 slice_bitcast_fusion.1
  1.4 0.1 broadcast_add_fusion
  1.5 0.1 iota_add_fusion
  1.6 0.6 convolution_convert_fusion
  2.2 0.3 copy.10
  2.5 0.0 copy-done.2
  2.5 0.0 copy-done.3
  2.6 0.1 copy.14
  2.7 0.8 pad_maximum_fusion.imgs
  3.5 0.7 reshape.110.refs
  4.1 44.8 %shard_map.68 = (bf16[16,5,16,512]{3,2,1,0:T(8,128)(2,1)}, bf16[32,7,8,128]{3,2,1,0:T(8,128)(2,1)}) custom-call(bf16[5,16,512]{2,1,0:T(8,128)(2,1)} %reshape.110.refs, bf16[32,7,8,128]{3,2,1,0:T(8,128)(2,1)} %pad_maximum_fusion.imgs), custom_call_target="tpu_custom_call" | custom-call | tf_op jit(solution)/shard_map/pallas_call | solution.py:108
  49.0 0.8 slice_bitcast_fusion
  49.8 0.1 copy.13
  49.9 0.6 convert_bitcast_fusion.meta
  50.5 9.6 %shard_map.69 = (bf16[9,256,512]{2,1,0:T(8,128)(2,1)}, f32[1536,256]{1,0:T(8,128)}) custom-call(bf16[1280,512]{1,0:T(8,128)(2,1)} %bitcast.23, bf16[32,7,8,128]{3,2,1,0:T(8,128)(2,1)} %get-tuple-element.11.imgs, s32[8,256]{1,0:T(8,128)} %convert_bitcast_fusion.meta), custom_call_target="tpu_custom_call" | custom-call | tf_op jit(solution)/shard_map/pallas_call | solution.py:330
  60.1 56.6 %shard_map.70 = (bf16[32,48,256]{2,1,0:T(8,128)(2,1)}, f32[32,8,256]{2,1,0:T(8,128)}) custom-call(f32[32,48,256]{2,1,0:T(8,128)} %bitcast.21, s32[8,256]{1,0:T(8,128)} %convert_bitcast_fusion.meta), custom_call_target="tpu_custom_call" | custom-call | tf_op jit(solution)/shard_map/pallas_call | solution.py:344
  116.7 8.5 %shard_map.71 = (bf16[1280,512]{1,0:T(8,128)(2,1)}, f32[8,256]{1,0:T(8,128)}) custom-call(bf16[32,48,256]{2,1,0:T(8,128)(2,1)} %get-tuple-element.13.like, f32[32,8,256]{2,1,0:T(8,128)} %get-tuple-element.14.stat, s32[8,256]{1,0:T(8,128)} %convert_bitcast_fusion.meta, bf16[9,256,512]{2,1,0:T(8,128)(2,1)} %get-tuple-element.15.shifted), custom_call_target="tpu_custom_call" | custom-call | tf_op jit(solution)/shard_map/pallas_call | solution.py:356
  125.2 31.3 %shard_map.72 = f32[5,16,512]{2,1,0:T(8,128)} custom-call(bf16[16,5,16,512]{3,2,1,0:T(8,128)(2,1)} %bitcast.24), custom_call_target="tpu_custom_call" | custom-call | tf_op jit(solution)/shard_map/pallas_call | solution.py:373
  156.5 1.6 %reshape.115 = f32[20,4,512]{2,1,0:T(4,128)} reshape(f32[5,16,512]{2,1,0:T(8,128)} %shard_map.72) | data formatting | bytes 327680 | tf_op jit(solution)/shard_map/reshape | solution.py:381
  158.1 0.7 slice.25
  158.8 0.6 dynamic-slice_bitcast_fusion
  (10 shorter events, 0.1 us)
Async XLA Ops:
  0.6 1.0 copy-start
  0.6 1.8 %copy-start.2 = (s32[8,2]{0,1:T(2,128)S(1)}, s32[8,2]{0,1:T(2,128)}, u32[]{:S(2)}) copy-start(s32[8,2]{0,1:T(2,128)} %param.8) | copy-start | bytes 196
  0.7 1.9 %copy-start.3 = (s32[8]{0:T(128)S(1)}, s32[8]{0:T(128)}, u32[]{:S(2)}) copy-start(s32[8]{0:T(128)} %param.7) | copy-start | bytes 100
  0.7 2.8 %copy-start.1 = (bf16[20,4,512]{2,1,0:T(4,128)(2,1)S(1)}, bf16[20,4,512]{2,1,0:T(4,128)(2,1)}, u32[]{:S(2)}) copy-start(bf16[20,4,512]{2,1,0:T(4,128)(2,1)} %param.9) | copy-start | bytes 245764

commit v2 on v1

--- a/solution.py
+++ b/solution.py
@@ -20,36 +20,40 @@
     )
 
 
-def greet(dom, ring):
+def signal_all(peers, ring):
     barrier = pltpu.get_barrier_semaphore()
     total = 0
-    if dom:
-        me = lax.axis_index("dom")
+    if peers is not None:
+        first, last, name = peers
 
         def one(k, carry):
-            pl.semaphore_signal(barrier, inc=1, device_id={"dom": lax.rem(me + k, dom)}, device_id_type=MESH)
+            pl.semaphore_signal(barrier, inc=1, device_id={"dom": name(k)}, device_id_type=MESH)
             return carry
 
-        lax.fori_loop(1, dom, one, 0)
-        total += dom - 1
+        lax.fori_loop(first, last, one, 0)
+        total += last - first
     if ring:
         z = lax.axis_index("cls")
         for step in (1, ring - 1):
             pl.semaphore_signal(barrier, inc=1, device_id={"cls": lax.rem(z + step, ring)}, device_id_type=MESH)
         total += 2
+    return barrier, total
+
+
+def greet(peers, ring):
+    barrier, total = signal_all(peers, ring)
     pl.semaphore_wait(barrier, total)
 
 
 def chunks(blocks):
-    half = (blocks + 1) // 2
-    return [(0, half), (half, blocks - half)]
+    return [(c, 1) for c in range(blocks)]
 
 
 def spread_kernel(dom, ring, refs, imgs, all_refs, all_imgs, rs, rr, ls, lr, ds, dr, local):
     d = lax.axis_index("dom")
     z = lax.axis_index("cls")
     right, left = lax.rem(z + 1, ring), lax.rem(z + ring - 1, ring)
-    greet(dom, ring)
+    greet((1, dom, lambda k: lax.rem(d + k, dom)), ring)
     parts = chunks(refs.shape[0])
     steps_r = ring // 2
     steps_l = ring - 1 - steps_r
@@ -67,7 +71,7 @@
         return remote(src, block, send.at[step, c], recv.at[step, c], {"cls": right if to_right else left})
 
     sent = {}
-    for c in range(2):
+    for c in range(len(parts)):
         for to_right in (True, False):
             sent[0, c, to_right] = hop(0, c, to_right)
             sent[0, c, to_right].start()
@@ -86,13 +90,13 @@
 
     lax.fori_loop(1, dom, start, 0)
     for step in range(1, steps_r):
-        for c in range(2):
+        for c in range(len(parts)):
             for to_right in (True, False):
                 if step < (steps_r if to_right else steps_l):
                     sent[step - 1, c, to_right].wait_recv()
                     sent[step, c, to_right] = hop(step, c, to_right)
                     sent[step, c, to_right].start()
-    for c in range(2):
+    for c in range(len(parts)):
         sent[steps_r - 1, c, True].wait_recv()
         sent[steps_l - 1, c, False].wait_recv()
     lax.fori_loop(1, dom, finish, 0)
@@ -113,7 +117,7 @@
         ),
         in_specs=[VMEM] * 2,
         out_specs=(VMEM, VMEM),
-        scratch_shapes=[sem((half, 2))] * 4 + [sem((dom,)), sem((dom,)), sem((2,))],
+        scratch_shapes=[sem((half, refs.shape[0]))] * 4 + [sem((dom,)), sem((dom,)), sem((2,))],
         compiler_params=pltpu.CompilerParams(collective_id=0, has_side_effects=True),
     )(refs, imgs)
 
@@ -164,33 +168,65 @@
         out[used:, :] = jnp.zeros((out.shape[0] - used, slots), jnp.float32)
 
 
-def evidence_kernel(dom, rotations, used, part, meta, like, stat, landed, s0, r0, s1, r1, s2, r2):
+def evidence_kernel(dom, rotations, used, part, meta, like, stat, held, landed, sems):
     d = lax.axis_index("dom")
-    greet(dom, 0)
-
-    def to(k):
-        return lax.rem(d + k, dom)
+    core = lax.rem(d, 2)
+    chip = d // 2
+    chips = dom // 2
+    other = chip * 2 + 1 - core
+
+    def at(k):
+        return lax.rem(chip + k, chips)
+
+    def back(k):
+        return lax.rem(chip + chips - k, chips)
+
+    barrier, total = signal_all((1, chips, lambda k: at(k) * 2 + core), 0)
+    pl.semaphore_signal(barrier, inc=1, device_id={"dom": other}, device_id_type=MESH)
+    pl.semaphore_wait(barrier, total + 1)
+
+    def swap(k):
+        return remote(part.at[at(k) * 2 + 1 - core], held.at[at(k)], sems.at[0, k], sems.at[1, k], {"dom": other})
 
     def scatter(k):
-        return remote(part.at[to(k)], landed.at[d], s0.at[k], r0.at[k], {"dom": to(k)})
-
-    def spread_like(k):
-        return remote(like.at[d], like.at[d], s1.at[k], r1.at[k], {"dom": to(k)})
-
-    def spread_stat(k):
-        return remote(stat.at[d], stat.at[d], s2.at[k], r2.at[k], {"dom": to(k)})
-
-    def start(k, carry):
-        scatter(k).start()
-        return carry
-
-    lax.fori_loop(1, dom, start, 0)
+        return remote(held.at[at(k)], landed.at[chip], sems.at[2, k], sems.at[3, k], {"dom": at(k) * 2 + core})
+
+    def across(ref, first, k):
+        return remote(ref.at[d], ref.at[d], sems.at[first, k], sems.at[first + 1, k], {"dom": at(k) * 2 + core})
+
+    def onward(ref, first, k):
+        block = ref.at[back(k) * 2 + core]
+        return remote(block, block, sems.at[first, k], sems.at[first + 1, k], {"dom": other})
+
+    def each(first, last, fn):
+        def body(k, carry):
+            fn(k)
+            return carry
+
+        lax.fori_loop(first, last, body, 0)
+
+    each(1, chips, lambda k: swap(k).start())
+    swap(0).start()
+
+    def merge(k):
+        swap(k).wait_recv()
+        held[at(k)] += part[at(k) * 2 + core]
+
+    merge(1)
+
+    def step(k):
+        merge(k)
+        scatter(k - 1).start()
+
+    each(2, chips, step)
+    merge(0)
+    scatter(chips - 1).start()
 
     def take(k, carry):
         scatter(k).wait_recv()
-        return carry + landed[lax.rem(d + dom - k, dom)]
-
-    total = lax.fori_loop(1, dom, take, part[d])
+        return carry + landed[back(k)]
+
+    total = lax.fori_loop(1, chips, take, held[chip])
     row = lax.broadcasted_iota(jnp.int32, total.shape, 0)
     prior = jnp.broadcast_to(meta[2:3, :], total.shape)
     delta = jnp.abs(row % rotations - prior)
@@ -203,21 +239,36 @@
     mass = jnp.sum(value, axis=0, keepdims=True)
     pick = lax.broadcasted_iota(jnp.int32, stat.shape[1:], 0)
     stat[d] = jnp.where(pick == 0, top, mass)
-
-    def give(k, carry):
+    each(0, chips, lambda k: swap(k).wait_send())
+
+    def give(k):
         scatter(k).wait_send()
-        spread_like(k).start()
-        spread_stat(k).start()
-        return carry
-
-    lax.fori_loop(1, dom, give, 0)
-
-    def finish(k, carry):
-        spread_like(k).wait()
-        spread_stat(k).wait()
-        return carry
-
-    lax.fori_loop(1, dom, finish, 0)
+        across(like, 4, k).start()
+        across(stat, 6, k).start()
+
+    each(1, chips, give)
+    onward(like, 8, 0).start()
+    onward(stat, 10, 0).start()
+
+    def relay(k):
+        across(like, 4, k).wait_recv()
+        onward(like, 8, k).start()
+        across(stat, 6, k).wait_recv()
+        onward(stat, 10, k).start()
+
+    each(1, chips, relay)
+
+    def finish(k):
+        onward(like, 8, k).wait()
+        onward(stat, 10, k).wait()
+
+    each(0, chips, finish)
+
+    def sent(k):
+        across(like, 4, k).wait_send()
+        across(stat, 6, k).wait_send()
+
+    each(1, chips, sent)
 
 
 def sums_kernel(groups, dim_j, like, stat, meta, shifted, out, evidence, post, dense, acc):
@@ -254,7 +305,7 @@
 def collect_kernel(ring, part, out, from_left, from_right, rs, rr, ls, lr):
     z = lax.axis_index("cls")
     right, left = lax.rem(z + 1, ring), lax.rem(z + ring - 1, ring)
-    greet(0, ring)
+    greet(None, ring)
     parts = chunks(part.shape[1])
     steps_r = ring // 2
     steps_l = ring - 1 - steps_r
@@ -345,11 +396,11 @@
         functools.partial(evidence_kernel, dom, rotations, 18 * dim_j),
         out_shape=(
             jax.ShapeDtypeStruct((dom, share, slots), jnp.bfloat16),
-            jax.ShapeDtypeStruct((dom, 8, slots), jnp.float32),
+            jax.ShapeDtypeStruct((dom, 2, slots), jnp.float32),
         ),
         in_specs=[VMEM] * 2,
         out_specs=(VMEM, VMEM),
-        scratch_shapes=[pltpu.VMEM((dom, share, slots), jnp.float32)] + [sem((dom,))] * 6,
+        scratch_shapes=[pltpu.VMEM((dom // 2, share, slots), jnp.float32)] * 2 + [sem((12, dom // 2))],
         compiler_params=pltpu.CompilerParams(collective_id=1, has_side_effects=True),
     )(part.reshape(dom, share, slots), meta)
 
@@ -375,7 +426,7 @@
         out_shape=jax.ShapeDtypeStruct(block, jnp.float32),
         in_specs=[VMEM],
         out_specs=VMEM,
-        scratch_shapes=[pltpu.VMEM((half,) + block, jnp.bfloat16)] * 2 + [sem((half, 2))] * 4,
+        scratch_shapes=[pltpu.VMEM((half,) + block, jnp.bfloat16)] * 2 + [sem((half, block[0]))] * 4,
         compiler_params=pltpu.CompilerParams(collective_id=2, has_side_effects=True),
     )(sums.reshape((ring,) + block))
     class_sums = total.reshape(references.shape[0], rotations, pixels).transpose(2, 0, 1)

time: 160 us -> 133 us (0.83)
  Pallas kernels: 151 us -> 124 us
    pallas_call x1, Pallas kernels: 56.6 us -> 29.8 us  [per_device(): pl.pallas_call(functools.partial(evidence_kernel, dom, rotations, 18 * di...]
where the time goes in v2:
time: 133 us
  Pallas kernels  124 us (93%)
  local copies, waits for them, and re-layouts  5.63 us (4%)
  other arithmetic  1.64 us (1%)
    pallas_call x1, Pallas kernels, spread(): pl.pallas_call(functools.partial(spread_kernel, dom, ring), out_shape=(ja...  43.5 us
    pallas_call x1, Pallas kernels, per_device(): pl.pallas_call(functools.partial(collect_kernel, ring), out_shape=jax.Sha...  32.8 us
    pallas_call x1, Pallas kernels, per_device(): pl.pallas_call(functools.partial(evidence_kernel, dom, rotations, 18 * di...  29.8 us
    pallas_call x1, Pallas kernels, per_device(): pl.pallas_call(functools.partial(score_kernel, ring, dim_j), out_shape=(j...  9.51 us
    pallas_call x1, Pallas kernels, per_device(): pl.pallas_call(functools.partial(sums_kernel, ring, dim_j), out_shape=(ja...  8.44 us

profile of v2, /device:TPU:24, one launch (start us, length us, event | category | flops | bytes accessed | tf_op | source)
XLA Modules:
  0.0 132.7 jit_solution(18273181670305049370)
XLA Ops:
  0.6 0.0 copy-start
  0.6 0.0 copy-start.2
  0.7 0.0 copy-start.3
  0.7 0.8 slice_bitcast_fusion.1
  1.4 0.1 broadcast_add_fusion
  1.5 0.1 iota_add_fusion
  1.6 0.6 convolution_convert_fusion
  2.2 0.3 copy.10
  2.5 0.0 copy-done.2
  2.5 0.0 copy-done.3
  2.6 0.1 copy.14
  2.7 0.8 pad_maximum_fusion.imgs
  3.5 0.7 reshape.110.refs
  4.1 43.5 %shard_map.68 = (bf16[16,5,16,512]{3,2,1,0:T(8,128)(2,1)}, bf16[32,7,8,128]{3,2,1,0:T(8,128)(2,1)}) custom-call(bf16[5,16,512]{2,1,0:T(8,128)(2,1)} %reshape.110.refs, bf16[32,7,8,128]{3,2,1,0:T(8,128)(2,1)} %pad_maximum_fusion.imgs), custom_call_target="tpu_custom_call" | custom-call | tf_op jit(solution)/shard_map/pallas_call | solution.py:112
  47.7 0.8 slice_bitcast_fusion
  48.5 0.1 copy.13
  48.6 0.6 convert_bitcast_fusion.meta
  49.2 9.5 %shard_map.69 = (bf16[9,256,512]{2,1,0:T(8,128)(2,1)}, f32[1536,256]{1,0:T(8,128)}) custom-call(bf16[1280,512]{1,0:T(8,128)(2,1)} %bitcast.23, bf16[32,7,8,128]{3,2,1,0:T(8,128)(2,1)} %get-tuple-element.11.imgs, s32[8,256]{1,0:T(8,128)} %convert_bitcast_fusion.meta), custom_call_target="tpu_custom_call" | custom-call | tf_op jit(solution)/shard_map/pallas_call | solution.py:381
  58.7 29.8 %shard_map.70 = (bf16[32,48,256]{2,1,0:T(8,128)(2,1)}, f32[32,2,256]{2,1,0:T(2,128)}) custom-call(f32[32,48,256]{2,1,0:T(8,128)} %bitcast.21, s32[8,256]{1,0:T(8,128)} %convert_bitcast_fusion.meta), custom_call_target="tpu_custom_call" | custom-call | tf_op jit(solution)/shard_map/pallas_call | solution.py:395
  88.5 8.4 %shard_map.71 = (bf16[1280,512]{1,0:T(8,128)(2,1)}, f32[8,256]{1,0:T(8,128)}) custom-call(bf16[32,48,256]{2,1,0:T(8,128)(2,1)} %get-tuple-element.13.like, f32[32,2,256]{2,1,0:T(2,128)} %get-tuple-element.14.stat, s32[8,256]{1,0:T(8,128)} %convert_bitcast_fusion.meta, bf16[9,256,512]{2,1,0:T(8,128)(2,1)} %get-tuple-element.15.shifted), custom_call_target="tpu_custom_call" | custom-call | tf_op jit(solution)/shard_map/pallas_call | solution.py:407
  97.0 32.8 %shard_map.72 = f32[5,16,512]{2,1,0:T(8,128)} custom-call(bf16[16,5,16,512]{3,2,1,0:T(8,128)(2,1)} %bitcast.24), custom_call_target="tpu_custom_call" | custom-call | tf_op jit(solution)/shard_map/pallas_call | solution.py:424
  129.8 1.6 %reshape.115 = f32[20,4,512]{2,1,0:T(4,128)} reshape(f32[5,16,512]{2,1,0:T(8,128)} %shard_map.72) | data formatting | bytes 327680 | tf_op jit(solution)/shard_map/reshape | solution.py:432
  131.4 0.7 slice.25
  132.1 0.6 dynamic-slice_bitcast_fusion
  (10 shorter events, 0.1 us)
Async XLA Ops:
  0.6 1.0 copy-start
  0.6 1.8 %copy-start.2 = (s32[8,2]{0,1:T(2,128)S(1)}, s32[8,2]{0,1:T(2,128)}, u32[]{:S(2)}) copy-start(s32[8,2]{0,1:T(2,128)} %param.8) | copy-start | bytes 196
  0.7 1.9 %copy-start.3 = (s32[8]{0:T(128)S(1)}, s32[8]{0:T(128)}, u32[]{:S(2)}) copy-start(s32[8]{0:T(128)} %param.7) | copy-start | bytes 100
  0.7 2.8 %copy-start.1 = (bf16[20,4,512]{2,1,0:T(4,128)(2,1)S(1)}, bf16[20,4,512]{2,1,0:T(4,128)(2,1)}, u32[]{:S(2)}) copy-start(bf16[20,4,512]{2,1,0:T(4,128)(2,1)} %param.9) | copy-start | bytes 245764

commit v3 on v2

v3 whole, which is shorter than its diff:
```python
import functools

import jax
import jax.numpy as jnp
from jax import lax
from jax.experimental import pallas as pl
from jax.experimental.pallas import tpu as pltpu
from jax.sharding import PartitionSpec as P

LAMBDA = 1.0
NEG_BIG = -1e30
LANES = 128
VMEM = pl.BlockSpec(memory_space=pltpu.VMEM)
MESH = pl.DeviceIdType.MESH


def remote(src, dst, send_sem, recv_sem, peer):
    return pltpu.make_async_remote_copy(
        src_ref=src, dst_ref=dst, send_sem=send_sem, recv_sem=recv_sem, device_id=peer, device_id_type=MESH
    )


def signal_all(peers, ring):
    barrier = pltpu.get_barrier_semaphore()
    total = 0
    if peers is not None:
        first, last, name = peers

        def one(k, carry):
            pl.semaphore_signal(barrier, inc=1, device_id={"dom": name(k)}, device_id_type=MESH)
            return carry

        lax.fori_loop(first, last, one, 0)
        total += last - first
    if ring:
        z = lax.axis_index("cls")
        for step in (1, ring - 1):
            pl.semaphore_signal(barrier, inc=1, device_id={"cls": lax.rem(z + step, ring)}, device_id_type=MESH)
        total += 2
    return barrier, total


def greet(peers, ring):
    barrier, total = signal_all(peers, ring)
    pl.semaphore_wait(barrier, total)


def chunks(blocks):
    return [(c, 1) for c in range(blocks)]


def each(first, last, fn):
    def body(k, carry):
        fn(k)
        return carry

    lax.fori_loop(first, last, body, 0)


def score_kernel(dom, ring, refs, imgs, shifted, out, meta, all_refs, all_imgs, score, rs, rr, ls, lr, ds, dr, local):
    d = lax.axis_index("dom")
    z = lax.axis_index("cls")
    right, left = lax.rem(z + 1, ring), lax.rem(z + ring - 1, ring)
    blocks, sixteen, pixels = refs.shape
    dim_j = blocks * sixteen
    strip, count, width = imgs.shape[1:]
    own_rows = strip - 3
    slots = dom * count
    steps_r = ring // 2
    steps_l = ring - 1 - steps_r
    greet((1, dom, lambda k: lax.rem(d + k, dom)), ring)
    own = pltpu.make_async_copy(refs, all_refs.at[z], local.at[0])
    own.start()
    mine = pltpu.make_async_copy(imgs.at[d], all_imgs.at[d], local.at[1])
    mine.start()

    def hop(step, c, to_right, src=None):
        piece = lax.rem(z + ring - step, ring) if to_right else lax.rem(z + step, ring)
        block = all_refs.at[piece, c]
        send, recv = (rs, rr) if to_right else (ls, lr)
        return remote(
            block if src is None else src, block, send.at[step, c], recv.at[step, c],
            {"cls": right if to_right else left},
        )

    for c in range(blocks):
        for to_right in (True, False):
            hop(0, c, to_right, refs.at[c]).start()

    def sent_strip(k):
        peer = lax.rem(d + k, dom)
        return remote(imgs.at[peer], all_imgs.at[d], ds.at[k], dr.at[k], {"dom": peer})

    each(1, dom, lambda k: sent_strip(k).start())
    out[...] = jnp.zeros_like(out)
    each(1, dom, lambda k: sent_strip(k).wait())
    mine.wait()
    own.wait()

    def forward(step, to_left):
        for c in range(blocks):
            hop(step - 1, c, True).wait_recv()
            hop(step, c, True).start()
            hop(step - 1, c, False).wait_recv()
            if to_left:
                hop(step, c, False).start()

    forward(1, True)
    lane = lax.broadcasted_iota(jnp.int32, (slots, width), 1)
    for h in range(own_rows + 2):
        mid = all_imgs[:, h].astype(jnp.float32).reshape(slots, width)
        before = jnp.where(lane == 0, 0.0, pltpu.roll(mid, 1, axis=1))
        after = jnp.where(lane == width - 1, 0.0, pltpu.roll(mid, width - 1, axis=1))
        for sy, plane in enumerate((before, mid, after)):
            plane = plane.astype(jnp.bfloat16)
            for sx in range(3):
                r = h - sx
                if 0 <= r < own_rows:
                    first = (3 * sx + sy) * slots
                    shifted[first:first + slots, r * width:(r + 1) * width] = plane
    notes = all_imgs[:, strip - 1].astype(jnp.float32).reshape(slots, width)
    meta[...] = jnp.transpose(notes)[:8].astype(jnp.int32)
    names = [jnp.broadcast_to(meta[t:t + 1, :], (dim_j, slots)) for t in range(2)]

    def pair(ga, gb):
        both = jnp.concatenate(
            [all_refs[ga].reshape(dim_j, pixels), all_refs[gb].reshape(dim_j, pixels)], axis=0
        )
        score[...] = lax.dot_general(
            both, shifted[...], (((1,), (1,)), ((), ())), preferred_element_type=jnp.float32
        )
        wide = both.astype(jnp.float32)
        bias = -0.5 * jnp.sum(wide * wide, axis=1, keepdims=True)

        def pick(w):
            cols = pl.ds(pl.multiple_of(w * slots, LANES), slots)
            first = score[0:dim_j, cols] + bias[:dim_j]
            second = score[dim_j:, cols] + bias[dim_j:]
            for t in range(2):
                rows = pl.ds(pl.multiple_of((t * 9 + w) * dim_j, 16), dim_j)
                out[rows, :] = jnp.where(
                    names[t] == ga, first, jnp.where(names[t] == gb, second, out[rows, :])
                )

        each(0, 9, pick)

    def near(step):
        pair(lax.rem(z + ring - step, ring), lax.rem(z + step, ring))

    near(1)

    def middle(step):
        forward(step, True)
        near(step)

    each(2, steps_l, middle)
    forward(steps_l, False)
    near(steps_l)
    for c in range(blocks):
        hop(steps_r - 1, c, True).wait_recv()
    pair(lax.rem(z + steps_r, ring), z)

    def drain(step):
        for c in range(blocks):
            hop(step, c, True).wait_send()

    def drain_left(step):
        for c in range(blocks):
            hop(step, c, False).wait_send()

    each(0, steps_r, drain)
    each(0, steps_l, drain_left)


def evidence_kernel(dom, rotations, used, part, meta, like, stat, held, landed, sems):
    d = lax.axis_index("dom")
    core = lax.rem(d, 2)
    chip = d // 2
    chips = dom // 2
    other = chip * 2 + 1 - core

    def at(k):
        return lax.rem(chip + k, chips)

    def back(k):
        return lax.rem(chip + chips - k, chips)

    barrier, total = signal_all((1, chips, lambda k: at(k) * 2 + core), 0)
    pl.semaphore_signal(barrier, inc=1, device_id={"dom": other}, device_id_type=MESH)
    pl.semaphore_wait(barrier, total + 1)

    def swap(k):
        return remote(part.at[at(k) * 2 + 1 - core], held.at[at(k)], sems.at[0, k], sems.at[1, k], {"dom": other})

    def scatter(k):
        return remote(held.at[at(k)], landed.at[chip], sems.at[2, k], sems.at[3, k], {"dom": at(k) * 2 + core})

    def across(ref, first, k):
        return remote(ref.at[d], ref.at[d], sems.at[first, k], sems.at[first + 1, k], {"dom": at(k) * 2 + core})

    def onward(ref, first, k):
        block = ref.at[back(k) * 2 + core]
        return remote(block, block, sems.at[first, k], sems.at[first + 1, k], {"dom": other})

    each(1, chips, lambda k: swap(k).start())
    swap(0).start()

    def merge(k):
        swap(k).wait_recv()
        held[at(k)] += part[at(k) * 2 + core]

    merge(1)

    def step(k):
        merge(k)
        scatter(k - 1).start()

    each(2, chips, step)
    merge(0)
    scatter(chips - 1).start()

    def take(k, carry):
        scatter(k).wait_recv()
        return carry + landed[back(k)]

    total = lax.fori_loop(1, chips, take, held[chip])
    row = lax.broadcasted_iota(jnp.int32, total.shape, 0)
    prior = jnp.broadcast_to(meta[2:3, :], total.shape)
    delta = jnp.abs(row % rotations - prior)
    dist = jnp.minimum(delta, rotations - delta).astype(jnp.float32)
    valid = row + d * total.shape[0] < used
    loglik = jnp.where(valid, total - LAMBDA * dist * dist, NEG_BIG)
    top = jnp.max(loglik, axis=0, keepdims=True)
    value = jnp.where(valid, jnp.exp(loglik - top), 0.0)
    like[d] = value.astype(jnp.bfloat16)
    mass = jnp.sum(value, axis=0, keepdims=True)
    pick = lax.broadcasted_iota(jnp.int32, stat.shape[1:], 0)
    stat[d] = jnp.where(pick == 0, top, mass)
    each(0, chips, lambda k: swap(k).wait_send())

    def give(k):
        scatter(k).wait_send()
        across(like, 4, k).start()
        across(stat, 6, k).start()

    each(1, chips, give)
    onward(like, 8, 0).start()
    onward(stat, 10, 0).start()

    def relay(k):
        across(like, 4, k).wait_recv()
        onward(like, 8, k).start()
        across(stat, 6, k).wait_recv()
        onward(stat, 10, k).start()

    each(1, chips, relay)

    def finish(k):
        onward(like, 8, k).wait()
        onward(stat, 10, k).wait()

    each(0, chips, finish)

    def sent(k):
        across(like, 4, k).wait_send()
        across(stat, 6, k).wait_send()

    each(1, chips, sent)


def sums_kernel(ring, like, stat, meta, shifted, out, evidence, post, dense, part, from_left, from_right, rs, rr, ls, lr):
    z = lax.axis_index("cls")
    right, left = lax.rem(z + 1, ring), lax.rem(z + ring - 1, ring)
    barrier, greetings = signal_all(None, ring)
    dom, rows, slots = like.shape
    blocks, sixteen, pixels = out.shape
    dim_j = blocks * sixteen
    steps_r = ring // 2
    steps_l = ring - 1 - steps_r
    top = stat[:, 0, :]
    mass = stat[:, 1, :]
    peak = jnp.max(top, axis=0, keepdims=True)
    total = jnp.sum(mass * jnp.exp(top - peak), axis=0, keepdims=True)
    ev = peak + jnp.log(total)
    evidence[...] = jnp.broadcast_to(ev, evidence.shape)

    def scale(k):
        factor = jnp.exp(stat[k, 0:1, :] - ev)
        post[pl.ds(pl.multiple_of(k * rows, 16), rows), :] = (like[k].astype(jnp.float32) * factor).astype(jnp.bfloat16)

    each(0, dom, scale)
    names = [jnp.broadcast_to(meta[t:t + 1, :], (dim_j, slots)) for t in range(2)]

    def pair(ga, gb):
        for w in range(9):
            p0 = post[w * dim_j:(w + 1) * dim_j, :].astype(jnp.float32)
            p1 = post[(9 + w) * dim_j:(10 + w) * dim_j, :].astype(jnp.float32)
            for first, g in ((0, ga), (dim_j, gb)):
                weight = jnp.where(names[0] == g, p0, jnp.where(names[1] == g, p1, 0.0))
                dense[first:first + dim_j, w * slots:(w + 1) * slots] = weight.astype(jnp.bfloat16)
        sums = jnp.dot(dense[...], shifted[...], preferred_element_type=jnp.float32).astype(jnp.bfloat16)
        part[ga] = sums[:dim_j].reshape(blocks, sixteen, pixels)
        part[gb] = sums[dim_j:].reshape(blocks, sixteen, pixels)

    def hop(step, c, to_right, src=None):
        hold, send, recv = (from_left, rs, rr) if to_right else (from_right, ls, lr)
        return remote(
            hold.at[step - 1, c] if src is None else src, hold.at[step, c], send.at[step, c], recv.at[step, c],
            {"cls": right if to_right else left},
        )

    def add_on(step, c, to_right, owner):
        hold = from_left if to_right else from_right
        hop(step - 1, c, to_right, part.at[owner, c]).wait_recv()
        hold[step - 1, c] = (
            hold[step - 1, c].astype(jnp.float32) + part[owner, c].astype(jnp.float32)
        ).astype(jnp.bfloat16)
        hop(step, c, to_right).start()

    far = lax.rem(z + steps_r, ring)
    pair(far, z)
    pl.semaphore_wait(barrier, greetings)
    for c in range(blocks):
        hop(0, c, True, part.at[far, c]).start()

    def owners(i):
        return lax.rem(z + steps_l - i, ring), lax.rem(z + ring - steps_l + i, ring)

    first_r, first_l = owners(0)
    pair(first_r, first_l)
    for c in range(blocks):
        hop(0, c, False, part.at[first_l, c]).start()
    for c in range(blocks):
        add_on(1, c, True, first_r)

    def step(i):
        owner_r, owner_l = owners(i)
        pair(owner_r, owner_l)
        for c in range(blocks):
            add_on(i, c, False, owner_l)
            add_on(i + 1, c, True, owner_r)

    each(1, steps_l, step)
    for c in range(blocks):
        hop(steps_r - 1, c, True).wait_recv()
        hop(steps_l - 1, c, False).wait_recv()
        out[c] = (
            part[z, c].astype(jnp.float32)
            + from_left[steps_r - 1, c].astype(jnp.float32)
            + from_right[steps_l - 1, c].astype(jnp.float32)
        )
    for to_right, steps in ((True, steps_r), (False, steps_l)):
        for c in range(blocks):
            hop(0, c, to_right, part.at[z, c]).wait_send()

        def drain(i):
            for c in range(blocks):
                hop(i, c, to_right).wait_send()

        each(1, steps, drain)


def per_device(particles, centers, rot_prior, groups, references):
    count, height, width = particles.shape
    dom = lax.axis_size("dom")
    ring = lax.axis_size("cls")
    rotations = references.shape[1]
    dim_j = references.shape[0] * rotations
    own_rows = height // dom
    pixels = own_rows * width
    strip = own_rows + 2
    slots = dom * count
    sem = pltpu.SemaphoreType.DMA

    line = jnp.arange(dom * strip, dtype=jnp.int32)
    line = (line // strip) * own_rows + line % strip - 1
    inside = (line >= 0) & (line < height)
    rows = jnp.arange(height, dtype=jnp.int32)
    cols = jnp.arange(width, dtype=jnp.int32)
    row_sel = (
        (rows[None, None, :] == line[None, :, None] + centers[:, 0, None, None]) & inside[None, :, None]
    ).astype(jnp.bfloat16)
    col_sel = (cols[None, None, :] == cols[None, :, None] + centers[:, 1, None, None]).astype(jnp.bfloat16)
    moved = jnp.einsum("kua,kav->kuv", row_sel, particles, preferred_element_type=jnp.float32).astype(jnp.bfloat16)
    strips = jnp.einsum("kub,kvb->kuv", moved, col_sel, preferred_element_type=jnp.float32).astype(jnp.bfloat16)
    strips = strips.reshape(count, dom, strip, width).transpose(1, 2, 0, 3)
    notes = jnp.concatenate([groups, rot_prior[:, None]], axis=1).astype(jnp.bfloat16)
    notes = jnp.pad(notes, ((0, 0), (0, width - notes.shape[1])))
    strips = jnp.concatenate([strips, jnp.broadcast_to(notes, (dom, 1, count, width))], axis=1)

    refs = references.reshape(dim_j // 16, 16, pixels)
    share = -(-18 * dim_j // (16 * dom)) * 16
    half = ring // 2
    block = refs.shape
    shifted, part, meta = pl.pallas_call(
        functools.partial(score_kernel, dom, ring),
        out_shape=(
            jax.ShapeDtypeStruct((9 * slots, pixels), jnp.bfloat16),
            jax.ShapeDtypeStruct((dom * share, slots), jnp.float32),
            jax.ShapeDtypeStruct((8, slots), jnp.int32),
        ),
        in_specs=[VMEM] * 2,
        out_specs=(VMEM, VMEM, VMEM),
        scratch_shapes=[
            pltpu.VMEM((ring,) + block, jnp.bfloat16),
            pltpu.VMEM(strips.shape, jnp.bfloat16),
            pltpu.VMEM((2 * dim_j, 9 * slots), jnp.float32),
        ]
        + [sem((half, block[0]))] * 4
        + [sem((dom,)), sem((dom,)), sem((2,))],
        compiler_params=pltpu.CompilerParams(collective_id=0, has_side_effects=True),
    )(refs, strips)

    like, stat = pl.pallas_call(
        functools.partial(evidence_kernel, dom, rotations, 18 * dim_j),
        out_shape=(
            jax.ShapeDtypeStruct((dom, share, slots), jnp.bfloat16),
            jax.ShapeDtypeStruct((dom, 2, slots), jnp.float32),
        ),
        in_specs=[VMEM] * 2,
        out_specs=(VMEM, VMEM),
        scratch_shapes=[pltpu.VMEM((dom // 2, share, slots), jnp.float32)] * 2 + [sem((12, dom // 2))],
        compiler_params=pltpu.CompilerParams(collective_id=1, has_side_effects=True),
    )(part.reshape(dom, share, slots), meta)

    total, evidence = pl.pallas_call(
        functools.partial(sums_kernel, ring),
        out_shape=(
            jax.ShapeDtypeStruct(block, jnp.float32),
            jax.ShapeDtypeStruct((8, slots), jnp.float32),
        ),
        in_specs=[VMEM] * 4,
        out_specs=(VMEM, VMEM),
        scratch_shapes=[
            pltpu.VMEM((dom * share, slots), jnp.bfloat16),
            pltpu.VMEM((2 * dim_j, 9 * slots), jnp.bfloat16),
            pltpu.VMEM((ring,) + block, jnp.bfloat16),
        ]
        + [pltpu.VMEM((half,) + block, jnp.bfloat16)] * 2
        + [sem((half, block[0]))] * 4,
        compiler_params=pltpu.CompilerParams(collective_id=2, has_side_effects=True),
    )(like, stat, meta, shifted)
    class_sums = total.reshape(references.shape[0], rotations, pixels).transpose(2, 0, 1)
    log_evidence = lax.dynamic_slice(evidence[0], (lax.axis_index("dom") * count,), (count,))
    return class_sums, log_evidence


def solution(mesh):
    placed = (
        P(("dom", "cls"), None, None),
        P(("dom", "cls"), None),
        P(("dom", "cls")),
        P(("dom", "cls"), None),
        P("cls", None, "dom"),
    )
    return jax.shard_map(
        per_device,
        mesh=mesh,
        in_specs=placed,
        out_specs=(P("dom", "cls", None), P(("dom", "cls"))),
        check_vma=False,
    )
```

time: 133 us -> 126 us (0.947)
  Pallas kernels: 124 us -> 116 us
    pallas_call x4 -> x2, Pallas kernels: 94.3 us -> 85.4 us  [the longest x1 52.5 us: per_device(): pl.pallas_call(functools.partial(score_kernel, dom, ring), out_shape=(jax...]
where the time goes in v3:
time: 126 us; the launch traced here: 125 us
  Pallas kernels  116 us (92%)
  local copies, waits for them, and re-layouts  4.74 us (4%)
  other arithmetic  2.35 us (2%)
    pallas_call x1, Pallas kernels, per_device(): pl.pallas_call(functools.partial(score_kernel, dom, ring), out_shape=(jax...  52.5 us
    pallas_call x1, Pallas kernels, per_device(): pl.pallas_call(functools.partial(sums_kernel, ring), out_shape=(jax.Shape...  32.9 us
    pallas_call x1, Pallas kernels, per_device(): pl.pallas_call(functools.partial(evidence_kernel, dom, rotations, 18 * di...  31.1 us

profile of v3, /device:TPU:24, one launch (start us, length us, event | category | flops | bytes accessed | tf_op | source)
XLA Modules:
  0.0 124.8 jit_solution(7723682168189777070)
XLA Ops:
  0.6 0.0 copy-start
  0.6 0.0 copy-start.1
  0.7 0.8 slice_bitcast_fusion
  1.4 0.1 broadcast_add_fusion
  1.5 0.1 iota_add_fusion
  1.6 0.0 copy-done
  1.6 0.6 convolution_convert_fusion
  2.2 0.3 copy.7
  2.5 0.7 convert.7
  3.2 0.7 convert_bitcast_fusion
  3.8 0.1 copy.9
  4.0 0.8 pad_maximum_fusion.imgs
  4.8 0.0 copy-done.1
  4.8 0.7 reshape.104.refs
  5.5 52.5 %shard_map.68 = (bf16[2304,512]{1,0:T(8,128)(2,1)}, f32[1536,256]{1,0:T(8,128)}, s32[8,256]{1,0:T(8,128)}) custom-call(bf16[5,16,512]{2,1,0:T(8,128)(2,1)} %reshape.104.refs, bf16[32,7,8,128]{3,2,1,0:T(8,128)(2,1)} %pad_maximum_fusion.imgs), custom_call_target="tpu_custom_call" | custom-call | tf_op jit(solution)/shard_map/pallas_call | solution.py:395
  57.9 31.1 %shard_map.69 = (bf16[32,48,256]{2,1,0:T(8,128)(2,1)}, f32[32,2,256]{2,1,0:T(2,128)}) custom-call(f32[32,48,256]{2,1,0:T(8,128)} %bitcast.14, s32[8,256]{1,0:T(8,128)} %get-tuple-element.10.meta), custom_call_target="tpu_custom_call" | custom-call | tf_op jit(solution)/shard_map/pallas_call | solution.py:414
  89.0 32.9 %shard_map.70 = (f32[5,16,512]{2,1,0:T(8,128)}, f32[8,256]{1,0:T(8,128)}) custom-call(bf16[32,48,256]{2,1,0:T(8,128)(2,1)} %get-tuple-element.11.like, f32[32,2,256]{2,1,0:T(2,128)} %get-tuple-element.12.stat, s32[8,256]{1,0:T(8,128)} %get-tuple-element.10.meta, bf16[2304,512]{1,0:T(8,128)(2,1)} %get-tuple-element.13.shifted), custom_call_target="tpu_custom_call" | custom-call | tf_op jit(solution)/shard_map/pallas_call | solution.py:426
  121.9 0.7 slice.17
  122.6 0.6 dynamic-slice_bitcast_fusion
  123.2 1.6 %reshape.107 = f32[20,4,512]{2,1,0:T(4,128)} reshape(f32[5,16,512]{2,1,0:T(8,128)} %get-tuple-element.14) | data formatting | bytes 327680 | tf_op jit(solution)/shard_map/reshape | solution.py:443
  (5 shorter events, 0.1 us)
Async XLA Ops:
  0.6 1.0 copy-start
  0.6 4.1 %copy-start.1 = (bf16[20,4,512]{2,1,0:T(4,128)(2,1)S(1)}, bf16[20,4,512]{2,1,0:T(4,128)(2,1)}, u32[]{:S(2)}) copy-start(bf16[20,4,512]{2,1,0:T(4,128)(2,1)} %param.9) | copy-start | bytes 245764

commit v4 on v3

--- a/solution.py
+++ b/solution.py
@@ -93,9 +93,6 @@
 
     each(1, dom, lambda k: sent_strip(k).start())
     out[...] = jnp.zeros_like(out)
-    each(1, dom, lambda k: sent_strip(k).wait())
-    mine.wait()
-    own.wait()
 
     def forward(step, to_left):
         for c in range(blocks):
@@ -106,6 +103,10 @@
                 hop(step, c, False).start()
 
     forward(1, True)
+    each(1, dom, lambda k: sent_strip(k).wait())
+    mine.wait()
+    own.wait()
+    forward(2, True)
     lane = lax.broadcasted_iota(jnp.int32, (slots, width), 1)
     for h in range(own_rows + 2):
         mid = all_imgs[:, h].astype(jnp.float32).reshape(slots, width)
@@ -147,15 +148,16 @@
     def near(step):
         pair(lax.rem(z + ring - step, ring), lax.rem(z + step, ring))
 
-    near(1)
+    forward(3, True)
+    each(1, 3, near)
 
     def middle(step):
         forward(step, True)
-        near(step)
-
-    each(2, steps_l, middle)
+        near(step - 1)
+
+    each(4, steps_l, middle)
     forward(steps_l, False)
-    near(steps_l)
+    each(steps_l - 1, steps_l + 1, near)
     for c in range(blocks):
         hop(steps_r - 1, c, True).wait_recv()
     pair(lax.rem(z + steps_r, ring), z)
@@ -282,7 +284,9 @@
     peak = jnp.max(top, axis=0, keepdims=True)
     total = jnp.sum(mass * jnp.exp(top - peak), axis=0, keepdims=True)
     ev = peak + jnp.log(total)
-    evidence[...] = jnp.broadcast_to(ev, evidence.shape)
+    count = evidence.shape[1]
+    turn = lax.rem(slots - lax.axis_index("dom") * count, slots)
+    evidence[...] = pltpu.roll(jnp.broadcast_to(ev, (8, slots)), turn, axis=1)[0:1, :count]
 
     def scale(k):
         factor = jnp.exp(stat[k, 0:1, :] - ev)
@@ -427,7 +431,7 @@
         functools.partial(sums_kernel, ring),
         out_shape=(
             jax.ShapeDtypeStruct(block, jnp.float32),
-            jax.ShapeDtypeStruct((8, slots), jnp.float32),
+            jax.ShapeDtypeStruct((1, count), jnp.float32),
         ),
         in_specs=[VMEM] * 4,
         out_specs=(VMEM, VMEM),
@@ -441,8 +445,7 @@
         compiler_params=pltpu.CompilerParams(collective_id=2, has_side_effects=True),
     )(like, stat, meta, shifted)
     class_sums = total.reshape(references.shape[0], rotations, pixels).transpose(2, 0, 1)
-    log_evidence = lax.dynamic_slice(evidence[0], (lax.axis_index("dom") * count,), (count,))
-    return class_sums, log_evidence
+    return class_sums, evidence.reshape(count)
 
 
 def solution(mesh):

time: 126 us -> 124 us (0.984)
  Pallas kernels: 116 us -> 113 us
    pallas_call x1, Pallas kernels: 52.5 us -> 49.2 us  [per_device(): pl.pallas_call(functools.partial(score_kernel, dom, ring), out_shape=(jax...]
where the time goes in v4:
time: 124 us; the launch traced here: 123 us
  Pallas kernels  113 us (91%)
  local copies, waits for them, and re-layouts  5.5 us (4%)
  other arithmetic  2.39 us (2%)
    pallas_call x1, Pallas kernels, per_device(): pl.pallas_call(functools.partial(score_kernel, dom, ring), out_shape=(jax...  49.2 us
    pallas_call x1, Pallas kernels, per_device(): pl.pallas_call(functools.partial(sums_kernel, ring), out_shape=(jax.Shape...  33.1 us
    pallas_call x1, Pallas kernels, per_device(): pl.pallas_call(functools.partial(evidence_kernel, dom, rotations, 18 * di...  31.2 us

profile of v4, /device:TPU:24, one launch (start us, length us, event | category | flops | bytes accessed | tf_op | source)
XLA Modules:
  0.0 122.6 jit_solution(1480076269158954446)
XLA Ops:
  0.6 0.0 copy-start
  0.6 0.7 convert_bitcast_fusion
  1.3 0.7 convert.7
  2.1 0.1 copy.9
  2.2 0.8 slice_bitcast_fusion
  2.9 0.1 iota_add_fusion
  3.0 0.1 broadcast_add_fusion
  3.1 1.5 %reshape.106.refs = bf16[5,16,512]{2,1,0:T(8,128)(2,1)} reshape(bf16[20,4,512]{2,1,0:T(4,128)(2,1)} %param.9) | data formatting | bytes 163840 | tf_op jit(solution)/shard_map/reshape | solution.py:395
  4.6 0.0 copy-done
  4.6 0.6 convolution_convert_fusion
  5.2 0.3 copy.7
  5.5 0.8 pad_maximum_fusion.imgs
  6.3 49.2 %shard_map.68 = (bf16[2304,512]{1,0:T(8,128)(2,1)}, f32[1536,256]{1,0:T(8,128)}, s32[8,256]{1,0:T(8,128)}) custom-call(bf16[5,16,512]{2,1,0:T(8,128)(2,1)} %reshape.106.refs, bf16[32,7,8,128]{3,2,1,0:T(8,128)(2,1)} %pad_maximum_fusion.imgs), custom_call_target="tpu_custom_call" | custom-call | tf_op jit(solution)/shard_map/pallas_call | solution.py:399
  55.5 31.2 %shard_map.69 = (bf16[32,48,256]{2,1,0:T(8,128)(2,1)}, f32[32,2,256]{2,1,0:T(2,128)}) custom-call(f32[32,48,256]{2,1,0:T(8,128)} %bitcast.13, s32[8,256]{1,0:T(8,128)} %get-tuple-element.10.meta), custom_call_target="tpu_custom_call" | custom-call | tf_op jit(solution)/shard_map/pallas_call | solution.py:418
  86.7 33.1 %shard_map.70 = (f32[5,16,512]{2,1,0:T(8,128)}, f32[1,8]{1,0:T(1,128)}) custom-call(bf16[32,48,256]{2,1,0:T(8,128)(2,1)} %get-tuple-element.11.like, f32[32,2,256]{2,1,0:T(2,128)} %get-tuple-element.12.stat, s32[8,256]{1,0:T(8,128)} %get-tuple-element.10.meta, bf16[2304,512]{1,0:T(8,128)(2,1)} %get-tuple-element.13.shifted), custom_call_target="tpu_custom_call" | custom-call | tf_op jit(solution)/shard_map/pallas_call | solution.py:430
  119.8 1.6 %reshape.109 = f32[20,4,512]{2,1,0:T(4,128)} reshape(f32[5,16,512]{2,1,0:T(8,128)} %get-tuple-element.14) | data formatting | bytes 327680 | tf_op jit(solution)/shard_map/reshape | solution.py:447
  121.4 1.2 copy.11
  (5 shorter events, 0.1 us)
Async XLA Ops:
  0.6 4.0 %copy-start = (bf16[8,128,128]{2,1,0:T(8,128)(2,1)S(1)}, bf16[8,128,128]{2,1,0:T(8,128)(2,1)}, u32[]{:S(2)}) copy-start(bf16[8,128,128]{2,1,0:T(8,128)(2,1)} %param.5) | copy-start | bytes 786436

commit v5 on v4

--- a/solution.py
+++ b/solution.py
@@ -57,7 +57,7 @@
     lax.fori_loop(first, last, body, 0)
 
 
-def score_kernel(dom, ring, refs, imgs, shifted, out, meta, all_refs, all_imgs, score, rs, rr, ls, lr, ds, dr, local):
+def score_kernel(dom, ring, refs, imgs, shifted, out, meta, all_refs, all_imgs, turned, score, rs, rr, ls, lr, ds, dr, local):
     d = lax.axis_index("dom")
     z = lax.axis_index("cls")
     right, left = lax.rem(z + 1, ring), lax.rem(z + ring - 1, ring)
@@ -108,17 +108,23 @@
     own.wait()
     forward(2, True)
     lane = lax.broadcasted_iota(jnp.int32, (slots, width), 1)
+    line = lax.broadcasted_iota(jnp.int32, (width, slots), 0)
     for h in range(own_rows + 2):
         mid = all_imgs[:, h].astype(jnp.float32).reshape(slots, width)
         before = jnp.where(lane == 0, 0.0, pltpu.roll(mid, 1, axis=1))
         after = jnp.where(lane == width - 1, 0.0, pltpu.roll(mid, width - 1, axis=1))
-        for sy, plane in enumerate((before, mid, after)):
+        mid_t = jnp.transpose(mid)
+        before_t = jnp.where(line == 0, 0.0, pltpu.roll(mid_t, 1, axis=0))
+        after_t = jnp.where(line == width - 1, 0.0, pltpu.roll(mid_t, width - 1, axis=0))
+        for sy, (plane, plane_t) in enumerate(((before, before_t), (mid, mid_t), (after, after_t))):
             plane = plane.astype(jnp.bfloat16)
+            plane_t = plane_t.astype(jnp.bfloat16)
             for sx in range(3):
                 r = h - sx
                 if 0 <= r < own_rows:
                     first = (3 * sx + sy) * slots
                     shifted[first:first + slots, r * width:(r + 1) * width] = plane
+                    turned[r * width:(r + 1) * width, first:first + slots] = plane_t
     notes = all_imgs[:, strip - 1].astype(jnp.float32).reshape(slots, width)
     meta[...] = jnp.transpose(notes)[:8].astype(jnp.int32)
     names = [jnp.broadcast_to(meta[t:t + 1, :], (dim_j, slots)) for t in range(2)]
@@ -127,9 +133,7 @@
         both = jnp.concatenate(
             [all_refs[ga].reshape(dim_j, pixels), all_refs[gb].reshape(dim_j, pixels)], axis=0
         )
-        score[...] = lax.dot_general(
-            both, shifted[...], (((1,), (1,)), ((), ())), preferred_element_type=jnp.float32
-        )
+        score[...] = jnp.dot(both, turned[...], preferred_element_type=jnp.float32)
         wide = both.astype(jnp.float32)
         bias = -0.5 * jnp.sum(wide * wide, axis=1, keepdims=True)
 
@@ -408,6 +412,7 @@
         scratch_shapes=[
             pltpu.VMEM((ring,) + block, jnp.bfloat16),
             pltpu.VMEM(strips.shape, jnp.bfloat16),
+            pltpu.VMEM((pixels, 9 * slots), jnp.bfloat16),
             pltpu.VMEM((2 * dim_j, 9 * slots), jnp.float32),
         ]
         + [sem((half, block[0]))] * 4

time: 124 us -> 123 us (level)
  no operation moved by 1% of the time
where the time goes in v5:
time: 123 us; the launch traced here: 122 us
  Pallas kernels  113 us (92%)
  local copies, waits for them, and re-layouts  5.5 us (4%)
  other arithmetic  2.39 us (2%)
    pallas_call x1, Pallas kernels, per_device(): pl.pallas_call(functools.partial(score_kernel, dom, ring), out_shape=(jax...  48.3 us
    pallas_call x1, Pallas kernels, per_device(): pl.pallas_call(functools.partial(sums_kernel, ring), out_shape=(jax.Shape...  33.6 us
    pallas_call x1, Pallas kernels, per_device(): pl.pallas_call(functools.partial(evidence_kernel, dom, rotations, 18 * di...  31.1 us

profile of v5, /device:TPU:24, one launch (start us, length us, event | category | flops | bytes accessed | tf_op | source)
XLA Modules:
  0.0 122.1 jit_solution(664477008202137087)
XLA Ops:
  0.6 0.0 copy-start
  0.6 0.7 convert_bitcast_fusion
  1.3 0.7 convert.7
  2.1 0.1 copy.9
  2.2 0.8 slice_bitcast_fusion
  2.9 0.1 iota_add_fusion
  3.0 0.1 broadcast_add_fusion
  3.1 1.5 %reshape.106.refs = bf16[5,16,512]{2,1,0:T(8,128)(2,1)} reshape(bf16[20,4,512]{2,1,0:T(4,128)(2,1)} %param.9) | data formatting | bytes 163840 | tf_op jit(solution)/shard_map/reshape | solution.py:399
  4.6 0.0 copy-done
  4.6 0.6 convolution_convert_fusion
  5.2 0.3 copy.7
  5.5 0.8 pad_maximum_fusion.imgs
  6.3 48.3 %shard_map.68 = (bf16[2304,512]{1,0:T(8,128)(2,1)}, f32[1536,256]{1,0:T(8,128)}, s32[8,256]{1,0:T(8,128)}) custom-call(bf16[5,16,512]{2,1,0:T(8,128)(2,1)} %reshape.106.refs, bf16[32,7,8,128]{3,2,1,0:T(8,128)(2,1)} %pad_maximum_fusion.imgs), custom_call_target="tpu_custom_call" | custom-call | tf_op jit(solution)/shard_map/pallas_call | solution.py:403
  54.7 31.1 %shard_map.69 = (bf16[32,48,256]{2,1,0:T(8,128)(2,1)}, f32[32,2,256]{2,1,0:T(2,128)}) custom-call(f32[32,48,256]{2,1,0:T(8,128)} %bitcast.13, s32[8,256]{1,0:T(8,128)} %get-tuple-element.10.meta), custom_call_target="tpu_custom_call" | custom-call | tf_op jit(solution)/shard_map/pallas_call | solution.py:423
  85.7 33.6 %shard_map.70 = (f32[5,16,512]{2,1,0:T(8,128)}, f32[1,8]{1,0:T(1,128)}) custom-call(bf16[32,48,256]{2,1,0:T(8,128)(2,1)} %get-tuple-element.11.like, f32[32,2,256]{2,1,0:T(2,128)} %get-tuple-element.12.stat, s32[8,256]{1,0:T(8,128)} %get-tuple-element.10.meta, bf16[2304,512]{1,0:T(8,128)(2,1)} %get-tuple-element.13.shifted), custom_call_target="tpu_custom_call" | custom-call | tf_op jit(solution)/shard_map/pallas_call | solution.py:435
  119.3 1.6 %reshape.109 = f32[20,4,512]{2,1,0:T(4,128)} reshape(f32[5,16,512]{2,1,0:T(8,128)} %get-tuple-element.14) | data formatting | bytes 327680 | tf_op jit(solution)/shard_map/reshape | solution.py:452
  120.9 1.2 copy.11
  (5 shorter events, 0.1 us)
Async XLA Ops:
  0.6 4.0 %copy-start = (bf16[8,128,128]{2,1,0:T(8,128)(2,1)S(1)}, bf16[8,128,128]{2,1,0:T(8,128)(2,1)}, u32[]{:S(2)}) copy-start(bf16[8,128,128]{2,1,0:T(8,128)(2,1)} %param.5) | copy-start | bytes 786436

commit v6 on v5

--- a/solution.py
+++ b/solution.py
@@ -10,6 +10,7 @@
 LAMBDA = 1.0
 NEG_BIG = -1e30
 LANES = 128
+STRIDE = 11
 VMEM = pl.BlockSpec(memory_space=pltpu.VMEM)
 MESH = pl.DeviceIdType.MESH
 
@@ -88,7 +89,7 @@
             hop(0, c, to_right, refs.at[c]).start()
 
     def sent_strip(k):
-        peer = lax.rem(d + k, dom)
+        peer = lax.rem(d + STRIDE * k, dom)
         return remote(imgs.at[peer], all_imgs.at[d], ds.at[k], dr.at[k], {"dom": peer})
 
     each(1, dom, lambda k: sent_strip(k).start())
@@ -186,10 +187,10 @@
     other = chip * 2 + 1 - core
 
     def at(k):
-        return lax.rem(chip + k, chips)
+        return lax.rem(chip + STRIDE * k, chips)
 
     def back(k):
-        return lax.rem(chip + chips - k, chips)
+        return lax.rem(chip + STRIDE * (chips - k), chips)
 
     barrier, total = signal_all((1, chips, lambda k: at(k) * 2 + core), 0)
     pl.semaphore_signal(barrier, inc=1, device_id={"dom": other}, device_id_type=MESH)

time: 123 us -> 122 us (level)
  the two profiles are of different devices: /device:TPU:24 before, /device:TPU:2 now
where the time goes in v6:
time: 122 us; the launch traced here: 121 us
  Pallas kernels  112 us (92%)
  local copies, waits for them, and re-layouts  5.5 us (5%)
  other arithmetic  2.39 us (2%)
    pallas_call x1, Pallas kernels, per_device(): pl.pallas_call(functools.partial(score_kernel, dom, ring), out_shape=(jax...  47.3 us
    pallas_call x1, Pallas kernels, per_device(): pl.pallas_call(functools.partial(sums_kernel, ring), out_shape=(jax.Shape...  33.6 us
    pallas_call x1, Pallas kernels, per_device(): pl.pallas_call(functools.partial(evidence_kernel, dom, rotations, 18 * di...  31.2 us

profile of v6, /device:TPU:2, one launch (start us, length us, event | category | flops | bytes accessed | tf_op | source)
XLA Modules:
  0.0 121.3 jit_solution(9952838127004492859)
XLA Ops:
  0.6 0.0 copy-start
  0.6 0.7 convert_bitcast_fusion
  1.3 0.7 convert.7
  2.1 0.1 copy.9
  2.2 0.8 slice_bitcast_fusion
  2.9 0.1 iota_add_fusion
  3.0 0.1 broadcast_add_fusion
  3.1 1.5 %reshape.106.refs = bf16[5,16,512]{2,1,0:T(8,128)(2,1)} reshape(bf16[20,4,512]{2,1,0:T(4,128)(2,1)} %param.9) | data formatting | bytes 163840 | tf_op jit(solution)/shard_map/reshape | solution.py:400
  4.6 0.0 copy-done
  4.6 0.6 convolution_convert_fusion
  5.2 0.3 copy.7
  5.5 0.8 pad_maximum_fusion.imgs
  6.3 47.3 %shard_map.68 = (bf16[2304,512]{1,0:T(8,128)(2,1)}, f32[1536,256]{1,0:T(8,128)}, s32[8,256]{1,0:T(8,128)}) custom-call(bf16[5,16,512]{2,1,0:T(8,128)(2,1)} %reshape.106.refs, bf16[32,7,8,128]{3,2,1,0:T(8,128)(2,1)} %pad_maximum_fusion.imgs), custom_call_target="tpu_custom_call" | custom-call | tf_op jit(solution)/shard_map/pallas_call | solution.py:404
  53.7 31.2 %shard_map.69 = (bf16[32,48,256]{2,1,0:T(8,128)(2,1)}, f32[32,2,256]{2,1,0:T(2,128)}) custom-call(f32[32,48,256]{2,1,0:T(8,128)} %bitcast.13, s32[8,256]{1,0:T(8,128)} %get-tuple-element.10.meta), custom_call_target="tpu_custom_call" | custom-call | tf_op jit(solution)/shard_map/pallas_call | solution.py:424
  84.9 33.6 %shard_map.70 = (f32[5,16,512]{2,1,0:T(8,128)}, f32[1,8]{1,0:T(1,128)}) custom-call(bf16[32,48,256]{2,1,0:T(8,128)(2,1)} %get-tuple-element.11.like, f32[32,2,256]{2,1,0:T(2,128)} %get-tuple-element.12.stat, s32[8,256]{1,0:T(8,128)} %get-tuple-element.10.meta, bf16[2304,512]{1,0:T(8,128)(2,1)} %get-tuple-element.13.shifted), custom_call_target="tpu_custom_call" | custom-call | tf_op jit(solution)/shard_map/pallas_call | solution.py:436
  118.5 1.6 %reshape.109 = f32[20,4,512]{2,1,0:T(4,128)} reshape(f32[5,16,512]{2,1,0:T(8,128)} %get-tuple-element.14) | data formatting | bytes 327680 | tf_op jit(solution)/shard_map/reshape | solution.py:453
  120.1 1.2 copy.11
  (5 shorter events, 0.1 us)
Async XLA Ops:
  0.6 4.0 %copy-start = (bf16[8,128,128]{2,1,0:T(8,128)(2,1)S(1)}, bf16[8,128,128]{2,1,0:T(8,128)(2,1)}, u32[]{:S(2)}) copy-start(bf16[8,128,128]{2,1,0:T(8,128)(2,1)} %param.5) | copy-start | bytes 786436
